TPU v7x, 512 devices: a whole 4x8x8 slice. The times are simulated.
512 devices in a mesh: ctx: 16 (over y_hi, x), head: 32 (over z, y_lo, core).
Axes of the slice: x: 4, y: 8 (y_hi: 4, y_lo: 2; y = y_hi * 2 + y_lo), z: 8, core: 2. Of those that a mesh axis runs over, the one named last changes fastest.
Arguments:
- tokens: float32 [8192, 1024], P(('ctx', 'head')), may hold values from -60 to 60
- norm_gain: float32 [1024], replicated, may hold values from 0.1 to 1.9
- w_query: float32 [1024, 8192], P(None, 'head'), may hold values from -0.125 to 0.125
- w_key: float32 [1024, 8192], P(None, 'head'), may hold values from -6 to 6
- w_value: float32 [1024, 8192], P(None, 'head'), may hold values from -0.1875 to 0.1875
- w_out: float32 [8192, 1024], P('head'), may hold values from -0.0625 to 0.0625
- shift_heads: int32 [64], P('head'), may hold values from 0 to 1, as said below
- cotangent: float32 [8192, 1024], P(('ctx', 'head')), may hold values from -6 to 6
Outputs:
- mixed: float32 [8192, 1024], P(('ctx', 'head'))
- input_grad: float32 [8192, 1024], P(('ctx', 'head'))
Inputs may be any that keep to these rules, and one draw needn't show every extreme that they name: For every i, exactly one of the heads 2i and 2i + 1 has shift_heads equal to 1.
All inputs are finite; a program needn't handle non-finite values.
Results may differ from a plain program's by a relative error of at most 0.0003.
Values sent between devices are 32-bit elements; how exact they have to be, the bound alone decides.
No kernel may reach another device: no remote copies, remote signals or barrier semaphores. Data moves between devices by JAX's collectives and lax.ppermute only.
A program may use at most 64 MiB of HBM per device.

v0:
```python
import math

import jax
import jax.numpy as jnp
from jax import lax
from jax.sharding import PartitionSpec as P

precise = lax.Precision.HIGHEST


def padded(block, sides, width):
    for axis, dim in sides:
        count = lax.axis_size(axis)
        forward = [(i, i + 1) for i in range(count - 1)]
        forward.append((count - 1, 0))
        backward = [(target, source) for source, target in forward]
        low = lax.ppermute(
            lax.slice_in_dim(block, block.shape[dim] - width, None, axis=dim), axis, forward
        )
        high = lax.ppermute(lax.slice_in_dim(block, 0, width, axis=dim), axis, backward)
        block = jnp.concatenate([low, block, high], axis=dim)
    return block


def from_behind(x, axis, by):
    length = lax.axis_size(axis)
    return lax.ppermute(x, axis, [(i, (i + by) % length) for i in range(length)])


def rms_rows(values, gain):
    return values * lax.rsqrt(jnp.mean(values * values, axis=-1, keepdims=True) + 1e-06) * gain


def softmax_last(scores):
    row_max = jnp.max(scores, axis=-1, keepdims=True)
    powers = jnp.exp(scores - row_max)
    return powers / jnp.sum(powers, axis=-1, keepdims=True)


def attend(query, keys, values, score_scale):
    probs = softmax_last(jnp.einsum("gqd,gkd->gqk", query, keys, precision=precise) * score_scale)
    return (probs, jnp.einsum("gqk,gkd->gqd", probs, values, precision=precise))


def attend_back(query, keys, values, probs, output, grad_out, score_scale):
    grad_values = jnp.einsum("gqk,gqd->gkd", probs, grad_out, precision=precise)
    grad_probs = jnp.einsum("gqd,gkd->gqk", grad_out, values, precision=precise)
    inner = jnp.sum(grad_out * output, axis=-1, keepdims=True)
    grad_scores = probs * (grad_probs - inner) * score_scale
    grad_query = jnp.einsum("gqk,gkd->gqd", grad_scores, keys, precision=precise)
    grad_keys = jnp.einsum("gqk,gqd->gkd", grad_scores, query, precision=precise)
    return (grad_query, grad_keys, grad_values)


def local(tokens, norm_gain, w_query, w_key, w_value, w_out, shift_heads, cotangent):
    gathered = lax.all_gather(tokens, "head", axis=0, tiled=True)
    group_len = gathered.shape[0]
    half_len = group_len // 2
    width = w_query.shape[1]
    head_dim = width // 2
    score_scale = 1.0 / math.sqrt(head_dim)
    normed = rms_rows(gathered, norm_gain)
    query = jnp.dot(normed, w_query, precision=precise)
    keys = jnp.dot(normed, w_key, precision=precise)
    values = jnp.dot(normed, w_value, precision=precise)
    second = shift_heads[1] == 1

    def split_heads(matrix):
        paired = matrix.reshape(group_len, 2, head_dim)
        moved = jnp.where(second, paired[:, 1], paired[:, 0])
        still = jnp.where(second, paired[:, 0], paired[:, 1])
        return (moved, still)

    def join_heads(moved, still):
        first_head = jnp.where(second, still, moved)
        second_head = jnp.where(second, moved, still)
        return jnp.stack([first_head, second_head], axis=1).reshape(group_len, width)

    query_moved, query_still = split_heads(query)
    keys_moved, keys_still = split_heads(keys)
    values_moved, values_still = split_heads(values)
    probs_still, out_still = attend(
        query_still[None], keys_still[None], values_still[None], score_scale
    )
    rim = padded(jnp.concatenate([keys_moved, values_moved], axis=1), (("ctx", 0),), half_len)
    keys_rim = rim[:, :head_dim].reshape(2, group_len, head_dim)
    values_rim = rim[:, head_dim : 2 * head_dim].reshape(2, group_len, head_dim)
    query_halves = query_moved.reshape(2, half_len, head_dim)
    probs_moved, out_moved = attend(query_halves, keys_rim, values_rim, score_scale)
    attention = join_heads(out_moved.reshape(group_len, head_dim), out_still[0])
    out_terms = jnp.dot(attention, w_out, precision=precise)
    mixed = tokens + lax.psum_scatter(out_terms, "head", scatter_dimension=0, tiled=True)
    cot_rows = lax.all_gather(cotangent, "head", axis=0, tiled=True)
    grad_attention = jnp.dot(cot_rows, w_out.T, precision=precise)
    grad_moved, grad_still = split_heads(grad_attention)
    grad_query_still, grad_keys_still, grad_values_still = attend_back(
        query_still[None],
        keys_still[None],
        values_still[None],
        probs_still,
        out_still,
        grad_still[None],
        score_scale,
    )
    grad_query_halves, grad_keys_rim, grad_values_rim = attend_back(
        query_halves,
        keys_rim,
        values_rim,
        probs_moved,
        out_moved,
        grad_moved.reshape(2, half_len, head_dim),
        score_scale,
    )
    grad_query_moved = grad_query_halves.reshape(group_len, head_dim)
    rim_grads = jnp.concatenate(
        [
            grad_keys_rim.reshape(2 * group_len, head_dim),
            grad_values_rim.reshape(2 * group_len, head_dim),
        ],
        axis=1,
    )
    from_right = from_behind(rim_grads[:half_len], "ctx", -1)
    from_left = from_behind(rim_grads[group_len + half_len :], "ctx", 1)
    own_rows = rim_grads[half_len : half_len + group_len] + jnp.concatenate(
        [from_left, from_right], axis=0
    )
    grad_keys_moved = own_rows[:, :head_dim]
    grad_values_moved = own_rows[:, head_dim:]
    grad_terms = jnp.dot(
        join_heads(grad_query_moved, grad_query_still[0]), w_query.T, precision=precise
    )
    grad_terms = grad_terms + jnp.dot(
        join_heads(grad_keys_moved, grad_keys_still[0]), w_key.T, precision=precise
    )
    grad_terms = grad_terms + jnp.dot(
        join_heads(grad_values_moved, grad_values_still[0]), w_value.T, precision=precise
    )
    grad_sum = lax.psum_scatter(grad_terms, "head", scatter_dimension=0, tiled=True)
    inverse = lax.rsqrt(jnp.mean(tokens * tokens, axis=-1, keepdims=True) + 1e-06)
    weighted = grad_sum * norm_gain
    correction = jnp.mean(weighted * tokens, axis=-1, keepdims=True)
    input_grad = (
        cotangent + weighted * inverse - tokens * (inverse * inverse * inverse) * correction
    )
    return (mixed, input_grad)


def solution(mesh):
    placed = (
        P(("ctx", "head"), None),
        P(),
        P(None, "head"),
        P(None, "head"),
        P(None, "head"),
        P("head", None),
        P("head"),
        P(("ctx", "head"), None),
    )
    return jax.shard_map(
        local,
        mesh=mesh,
        in_specs=placed,
        out_specs=(P(("ctx", "head"), None), P(("ctx", "head"), None)),
        check_vma=False,
    )
```

profile of v0, /device:TPU:6, one launch (start us, length us, event | category | flops | bytes accessed | tf_op | source)
XLA Modules:
  0.0 502.4 jit_solution(17327788818730543394)
XLA Ops:
  8.7 1.2 slice.62
  10.6 71.7 %all-gather.5.cloned.1.call-done = f32[512,1024]{1,0:T(8,128)} async-done(((f32[16,1024]{1,0:T(8,128)}), f32[512,1024]{1,0:T(8,128)}) %all-gather.5.cloned.1.call-update) | async-done | bytes 2097168 | tf_op jit(solution)/shard_map/all_gather | solution.py:93
  82.3 3.8 fusion.44
  86.2 0.8 copy.53
  87.0 64.3 %all-gather.3.cloned.1.call-done = f32[512,1024]{1,0:T(8,128)} async-done(((f32[16,1024]{1,0:T(8,128)}), f32[512,1024]{1,0:T(8,128)}) %all-gather.3.cloned.1.call-update) | async-done | bytes 2097168 | tf_op jit(solution)/shard_map/all_gather | solution.py:56
  151.3 2.0 multiply_reduce_fusion
  153.3 0.8 copy.52
  154.1 3.6 fusion
  158.4 1.8 copy.51
  160.2 0.8 copy.50
  161.1 3.6 fusion.1
  165.4 0.8 copy.49
  166.2 2.3 fusion.2
  170.6 0.9 fusion.21
  171.5 4.3 collective-permute-start
  175.8 2.5 collective-permute-start.1
  178.3 1.1 fusion.39
  180.4 3.4 online-softmax
  184.6 10.3 %collective-permute-done.1 = f32[256,256]{1,0:T(8,128)} collective-permute-done((f32[256,256]{1,0:T(8,128)}, f32[256,256]{1,0:T(8,128)}, u32[]{:S(2)}, u32[]{:S(2)}) %collective-permute-start.1) | collective-permute-done | bytes 262176 | tf_op jit(solution)/shard_map/ppermute | solution.py:20
  194.9 1.2 pad_maximum_fusion
  196.1 0.9 fusion.34
  197.0 1.1 fusion.40
  199.0 3.5 online-softmax.1
  202.5 1.2 multiply_reduce_fusion.1
  203.7 3.4 fusion.19
  207.2 1.1 fusion.4
  208.3 1.1 fusion.45
  209.4 1.9 fusion.47
  212.0 1.9 collective-permute-start.2
  213.9 4.1 collective-permute-start.3
  218.1 0.9 fusion.26
  219.0 1.1 fusion.6
  220.1 1.0 bitcast_select_fusion.1
  221.9 2.0 copy.31
  224.0 5.9 %fusion.46 = f32[512,1024]{1,0:T(8,128)} fusion(f32[512,256]{0,1:T(8,128)} %bitcast.97, f32[1024,256]{1,0:T(8,128)S(1)} %copy-done), kind=kOutput, calls=%fused_computation.89 | convolution fusion | flops 1610612736 | bytes 3670016 | tf_op jit(solution)/shard_map/dot_general | solution.py:129
  229.9 2.0 fusion.23
  231.9 1.1 fusion.18
  233.0 2.6 select_bitcast_fusion.1
  235.7 1.0 copy.39
  236.7 1.0 pad_maximum_fusion.3
  237.9 3.7 fusion.48
  241.7 5.0 add_add_fusion
  246.7 0.9 copy-done.34
  248.1 3.2 fusion.43
  251.3 119.4 %reduce-scatter.5.cloned.1.call-done = f32[16,1024]{1,0:T(8,128)} async-done(((f32[512,1024]{1,0:T(8,128)}), f32[16,1024]{1,0:T(8,128)}) %reduce-scatter.5.cloned.1.call-update) | async-done | bytes 65552 | tf_op jit(solution)/shard_map/reduce_scatter | solution.py:138
  370.7 1.0 multiply_reduce_fusion.3
  371.6 122.4 %reduce-scatter.3.cloned.1.call-done = f32[16,1024]{1,0:T(8,128)} async-done(((f32[512,1024]{1,0:T(8,128)}), f32[16,1024]{1,0:T(8,128)}) %reduce-scatter.3.cloned.1.call-update) | async-done | bytes 65552 | tf_op jit(solution)/shard_map/reduce_scatter | solution.py:92
  494.1 1.6 multiply_subtract_fusion
  (114 shorter events, 10.1 us)
Async XLA Ops:
  7.2 159.1 %copy-start = (f32[1024,256]{1,0:T(8,128)S(1)}, f32[1024,256]{1,0:T(8,128)}, u32[]{:S(2)}) copy-start(f32[1024,256]{1,0:T(8,128)} %param.10) | copy-start | bytes 3145732
  7.2 75.1 %all-gather.5.cloned.1.call-start = ((), (), s32[]{:S(2)}) async-start(), calls=%async_computation.4 | async-start | bytes 2162688 | tf_op jit(solution)/shard_map/all_gather | solution.py:93
  7.9 143.4 %all-gather.3.cloned.1.call-start = ((), (), s32[]{:S(2)}) async-start(), calls=%async_computation.2 | async-start | bytes 2162688 | tf_op jit(solution)/shard_map/all_gather | solution.py:56
  8.7 362.0 %reduce-scatter.5.cloned.1.call-start = ((), (), s32[]{:S(2)}) async-start(), calls=%async_computation.5 | async-start | bytes 2162688 | tf_op jit(solution)/shard_map/reduce_scatter | solution.py:138
  86.1 68.0 %copy-start.41 = (f32[1024]{0:T(1024)S(1)}, f32[1024]{0:T(1024)}, u32[]{:S(2)}) copy-start(f32[1024]{0:T(1024)} %param.9) | copy-start | bytes 12292
  151.3 2.8 copy-start.1
  168.6 1.1 copy-start.10
  168.6 1.1 copy-start.29
  168.6 1.2 copy-start.31
  168.9 14.8 %copy-start.8 = (f32[512,1,128]{2,0,1:T(8,128)}, f32[512,1,128]{2,0,1:T(8,128)S(1)}, u32[]{:S(2)}) copy-start(f32[512,1,128]{2,0,1:T(8,128)S(1)} %copy.46) | copy-start | bytes 786436
  169.7 9.7 %copy-start.12 = (f32[512,1,128]{2,0,1:T(8,128)}, f32[512,1,128]{2,0,1:T(8,128)S(1)}, u32[]{:S(2)}) copy-start(f32[512,1,128]{2,0,1:T(8,128)S(1)} %copy.48) | copy-start | bytes 786436
  170.6 9.1 %copy-start.21 = (f32[512,128]{1,0:T(8,128)}, f32[512,128]{1,0:T(8,128)S(1)}, u32[]{:S(2)}) copy-start(f32[512,128]{1,0:T(8,128)S(1)} %get-tuple-element.24) | copy-start | bytes 786436
  170.6 9.1 %copy-start.23 = (f32[512,128]{1,0:T(8,128)}, f32[512,128]{1,0:T(8,128)S(1)}, u32[]{:S(2)}) copy-start(f32[512,128]{1,0:T(8,128)S(1)} %get-tuple-element.42) | copy-start | bytes 786436
  171.5 13.2 %collective-permute-start = (f32[256,256]{1,0:T(8,128)}, f32[256,256]{1,0:T(8,128)}, u32[]{:S(2)}, u32[]{:S(2)}) collective-permute-start(f32[256,256]{1,0:T(8,128)} %get-tuple-element.22), channel_id=1, source_target_pairs={{0,32},{32,64},{64,96},{96,128},{128,160},{160,192},{192,224},{224... | collective-permute-start | bytes 786440 | tf_op jit(solution)/shard_map/ppermute | solution.py:17
  175.8 8.0 %copy-start.19 = (f32[512,1,128]{2,0,1:T(8,128)S(1)}, f32[512,1,128]{2,0,1:T(8,128)}, u32[]{:S(2)}) copy-start(f32[512,1,128]{2,0,1:T(8,128)} %copy.53) | copy-start | bytes 786436
  175.8 19.1 %collective-permute-start.1 = (f32[256,256]{1,0:T(8,128)}, f32[256,256]{1,0:T(8,128)}, u32[]{:S(2)}, u32[]{:S(2)}) collective-permute-start(f32[256,256]{1,0:T(8,128)} %get-tuple-element.23), channel_id=1, source_target_pairs={{32,0},{64,32},{96,64},{128,96},{160,128},{192,160},{224,192},{256... | collective-permute-start | bytes 786440 | tf_op jit(solution)/shard_map/ppermute | solution.py:20
  179.4 1.0 copy-start.4
  180.4 14.5 %copy-start.22 = (f32[512,128]{1,0:T(8,128)S(1)}, f32[512,128]{1,0:T(8,128)}, u32[]{:S(2)}) copy-start(f32[512,128]{1,0:T(8,128)} %copy-done.21) | copy-start | bytes 786436
  198.0 1.0 copy-start.2
  203.7 3.4 copy-start.3
  203.7 3.4 copy-start.26
  203.7 3.4 copy-start.30
  207.1 4.1 copy-start.24
  209.3 8.7 %copy-start.18 = (f32[2,256,128]{2,1,0:T(8,128)S(1)}, f32[2,256,128]{2,1,0:T(8,128)}, u32[]{:S(2)}) copy-start(f32[2,256,128]{2,1,0:T(8,128)} %online-softmax.1) | copy-start | bytes 786436
  209.4 8.7 %copy-start.20 = (f32[512,1,128]{2,0,1:T(8,128)S(1)}, f32[512,1,128]{2,0,1:T(8,128)}, u32[]{:S(2)}) copy-start(f32[512,1,128]{2,0,1:T(8,128)} %copy.52) | copy-start | bytes 786436
  209.4 8.7 %copy-start.36 = (f32[512,128]{1,0:T(8,128)S(1)}, f32[512,128]{1,0:T(8,128)}, u32[]{:S(2)}) copy-start(f32[512,128]{1,0:T(8,128)} %online-softmax) | copy-start | bytes 786436
  211.2 7.7 %copy-start.5 = (f32[512,512]{1,0:T(8,128)S(1)}, f32[512,512]{1,0:T(8,128)}, u32[]{:S(2)}) copy-start(f32[512,512]{1,0:T(8,128)} %copy-done.4) | copy-start | bytes 3145732
  211.2 7.7 %copy-start.33 = (f32[512,128]{1,0:T(8,128)S(1)}, f32[512,128]{1,0:T(8,128)}, u32[]{:S(2)}) copy-start(f32[512,128]{1,0:T(8,128)} %get-tuple-element.25) | copy-start | bytes 786436
  212.0 19.9 %collective-permute-start.2 = (f32[256,256]{1,0:T(8,128)}, f32[256,256]{1,0:T(8,128)}, u32[]{:S(2)}, u32[]{:S(2)}) collective-permute-start(f32[256,256]{1,0:T(8,128)} %get-tuple-element.6), channel_id=1, source_target_pairs={{0,32},{32,64},{64,96},{96,128},{128,160},{160,192},{192,224},{224... | collective-permute-start | bytes 786440 | tf_op jit(solution)/shard_map/ppermute | solution.py:27
  213.9 18.0 %collective-permute-start.3 = (f32[256,256]{1,0:T(8,128)S(1)}, f32[256,256]{1,0:T(8,128)}, u32[]{:S(2)}, u32[]{:S(2)}) collective-permute-start(f32[256,256]{1,0:T(8,128)S(1)} %get-tuple-element.7), channel_id=1, source_target_pairs={{0,480},{32,0},{64,32},{96,64},{128,96},{160,128},{192,160},{224,1... | collective-permute-start | bytes 786440 | tf_op jit(solution)/shard_map/ppermute | solution.py:27
  218.9 1.2 copy-start.39
  218.9 1.2 copy-start.11
  218.9 1.2 copy-start.13
  220.1 1.0 copy-start.16
  224.0 5.9 %copy-start.40 = (f32[512,1,128]{2,0,1:T(8,128)S(1)}, f32[512,1,128]{2,0,1:T(8,128)}, u32[]{:S(2)}) copy-start(f32[512,1,128]{2,0,1:T(8,128)} %copy-done.39) | copy-start | bytes 786436
  229.9 2.0 copy-start.25
  229.9 3.1 copy-start.9
  229.9 3.1 copy-start.17
  235.6 1.0 copy-start.28
  235.6 2.3 copy-start.14
  237.9 3.7 copy-start.6
  237.9 3.7 copy-start.15
  237.9 3.7 copy-start.27
  246.7 1.0 copy-start.35
  246.7 1.4 copy-start.7
  246.7 247.4 %reduce-scatter.3.cloned.1.call-start = ((), (), s32[]{:S(2)}) async-start(), calls=%async_computation.3 | async-start | bytes 2162688 | tf_op jit(solution)/shard_map/reduce_scatter | solution.py:92
  248.1 122.6 %copy-start.37 = (f32[16,1024]{1,0:T(8,128)S(1)}, f32[16,1024]{1,0:T(8,128)}, u32[]{:S(2)}) copy-start(f32[16,1024]{1,0:T(8,128)} %param.8) | copy-start | bytes 196612
  248.1 246.0 %copy-start.38 = (f32[16,1024]{1,0:T(8,128)S(1)}, f32[16,1024]{1,0:T(8,128)}, u32[]{:S(2)}) copy-start(f32[16,1024]{1,0:T(8,128)} %param.15) | copy-start | bytes 196612
  (2 other events, 1.9 us)
Sparse Core Ops, SparseCore 0:
  10.1 72.1 all-gather.4
  84.4 66.8 all-gather.2
  246.8 123.7 reduce-scatter.4
  373.3 120.7 reduce-scatter.2
where the time goes:
time: 511 us; the launch traced here: 502 us
  waiting for transfers between devices  390 us (76%)
  matrix products  47.4 us (9%)
  local copies, waits for them, and re-layouts  15.9 us (3%)
  between operations  15.3 us (3%)
  other arithmetic  14.5 us (3%)
  starting transfers between devices  13 us (3%)
  Pallas kernels  6.87 us (1%)
    reduce_scatter x1, waiting for transfers between devices, local(): lax.psum_scatter(out_terms, 'head', scatter_dimension=0, tiled=True)  122 us
    reduce_scatter x1, waiting for transfers between devices, local(): lax.psum_scatter(grad_terms, 'head', scatter_dimension=0, tiled=True)  119 us
    all_gather x1, waiting for transfers between devices, local(): cot_rows = lax.all_gather(cotangent, 'head', axis=0, tiled=True)  71.7 us
    all_gather x1, waiting for transfers between devices, local(): gathered = lax.all_gather(tokens, 'head', axis=0, tiled=True)  64.3 us
    ppermute x1, waiting for transfers between devices, padded(): lax.ppermute(lax.slice_in_dim(block, 0, width, axis=dim), axis, backward)  10.3 us
  transfers between devices with their start and end apart: 8, of which 6 were waited for; matrix products, arithmetic and copies ran while one was open for 5% of the time, Pallas kernels for 1%

commit v1 on v0

v1 whole, which is shorter than its diff:
```python
import functools
import math

import jax
import jax.numpy as jnp
from jax import lax
from jax.experimental import pallas as pl
from jax.experimental.pallas import tpu as pltpu
from jax.sharding import PartitionSpec as P

F32, BF16 = jnp.float32, jnp.bfloat16
NN, NT, TN = ((1,), (0,)), ((1,), (1,)), ((0,), (0,))


def parts2(x):
    high = x.astype(BF16)
    return high, (x - high.astype(F32)).astype(BF16)


def parts3(x):
    high = x.astype(BF16)
    rest = x - high.astype(F32)
    middle = rest.astype(BF16)
    return high, middle, (rest - middle.astype(F32)).astype(BF16)


def mul(a, b, dims):
    return lax.dot_general(a, b, (dims, ((), ())), preferred_element_type=F32)


def mul3(a, b, dims):
    return mul(a[0], b[0], dims) + (mul(a[0], b[1], dims) + mul(a[1], b[0], dims))


def mul6(a, b, dims):
    small = mul(a[1], b[1], dims) + mul(a[0], b[2], dims) + mul(a[2], b[0], dims)
    return mul(a[0], b[0], dims) + (mul(a[0], b[1], dims) + mul(a[1], b[0], dims) + small)


def cat(a, b):
    return jnp.concatenate([a, b], axis=1)


def scores6(a, b):
    (ah, am, al), (bh, bm, bl) = a, b
    wide = cat(bh, bm)
    return mul(cat(ah, ah), wide, NT) + (mul(cat(am, am), wide, NT) + mul(cat(ah, al), cat(bl, bh), NT))


def scores3(a, b):
    (ah, am), (bh, bm) = a, b
    return mul(cat(ah, am), cat(bh, bh), NT) + mul(ah, bm, NT)


def weigh3(a, b, dims):
    width = b[0].shape[1]
    both = mul(a[0], cat(b[0], b[1]), dims)
    return both[:, :width] + (both[:, width:] + mul(a[1], b[0], dims))


def head_cols(flag_ref, width):
    second = flag_ref[0]
    moved = pl.multiple_of(second * width, width)
    still = pl.multiple_of((1 - second) * width, width)
    return pl.ds(moved, width), pl.ds(still, width)


def normed_parts(own_ref, other_ref, gain_ref, refs):
    rows = own_ref.shape[1]
    for slot, source in enumerate((own_ref, other_ref)):

        @pl.loop(0, 2)
        def _(half):
            x = source[half]
            x = x * lax.rsqrt(jnp.mean(x * x, axis=-1, keepdims=True) + 1e-06) * gain_ref[...]
            at = pl.ds(pl.multiple_of((2 * half + slot) * rows, rows), rows)
            for ref, part in zip(refs, parts3(x)):
                ref[at] = part


def softmax_rows(scores):
    powers = jnp.exp(scores - jnp.max(scores, axis=-1, keepdims=True))
    return powers / jnp.sum(powers, axis=-1, keepdims=True)


def rim_kernel(flag_ref, own_ref, other_ref, gain_ref, wk_ref, wv_ref, first_ref, last_ref, nh, nm, nl):
    normed_parts(own_ref, other_ref, gain_ref, (nh, nm, nl))
    moved, _ = head_cols(flag_ref, wk_ref.shape[1] // 2)
    half = first_ref.shape[0]
    both = mul6((nh[...], nm[...], nl[...]), parts3(cat(wk_ref[:, moved], wv_ref[:, moved])), NN)
    first_ref[...] = both[:half]
    last_ref[...] = both[half:]


def still_kernel(scale, flag_ref, own_ref, other_ref, gain_ref, wq_ref, wk_ref, wv_ref, q_ref, kv_ref, ps_ref, os_ref, nh, nm, nl):
    normed_parts(own_ref, other_ref, gain_ref, (nh, nm, nl))
    hd = wk_ref.shape[1] // 2
    _, still = head_cols(flag_ref, hd)
    n = (nh[...], nm[...], nl[...])
    q_ref[...] = mul6(n, parts3(wq_ref[...]), NN)
    kv_ref[...] = mul6(n, parts3(cat(wk_ref[:, still], wv_ref[:, still])), NN)
    scores = scores6(parts3(q_ref[:, still]), parts3(kv_ref[:, :hd])) * scale
    probs = softmax_rows(scores)
    ps_ref[...] = probs
    os_ref[...] = weigh3(parts2(probs), parts2(kv_ref[:, hd:]), NN)


def moved_kernel(scale, flag_ref, q_ref, first_ref, last_ref, low_ref, high_ref, os_ref, wo_ref, pm_ref, mine_ref, theirs_ref, both):
    hd = os_ref.shape[1]
    half = first_ref.shape[0]
    moved, still = head_cols(flag_ref, hd)
    for g, (a_ref, b_ref) in enumerate(((low_ref, first_ref), (last_ref, high_ref))):
        rim = jnp.concatenate([a_ref[...], b_ref[...]], axis=0)
        at = pl.ds(g * half, half)
        scores = scores6(parts3(q_ref[at, moved]), parts3(rim[:, :hd])) * scale
        probs = softmax_rows(scores)
        pm_ref[g] = probs
        both[at, moved] = weigh3(parts2(probs), parts2(rim[:, hd:]), NN)
    both[:, still] = os_ref[...]
    rows = mine_ref.shape[1]
    out = mul3(parts2(both[...]), parts2(wo_ref[...]), NN)
    for g in range(2):
        mine_ref[g] = out[2 * g * rows : (2 * g + 1) * rows]
        theirs_ref[g] = out[(2 * g + 1) * rows : (2 * g + 2) * rows]


def group_back(query, kv, probs, grad_out, scale):
    hd = query.shape[1]
    q, k, v, g = parts2(query), parts2(kv[:, :hd]), parts2(kv[:, hd:]), parts2(grad_out)
    grad_probs = scores3(g, v)
    inner = jnp.sum(probs * grad_probs, axis=-1, keepdims=True)
    grad_values = weigh3(parts2(probs), g, TN)
    grad_scores = parts2(probs * (grad_probs - inner) * scale)
    grad_query = weigh3(grad_scores, k, NN)
    grad_keys = weigh3(grad_scores, q, TN)
    return grad_query, cat(grad_keys, grad_values)


def moved_back_kernel(scale, flag_ref, own_ref, other_ref, wo_ref, q_ref, first_ref, last_ref, low_ref, high_ref, pm_ref, ga_ref, dq_ref, left_ref, right_ref, keep_ref, ch, cm):
    hd = q_ref.shape[1] // 2
    half = first_ref.shape[0]
    rows = own_ref.shape[1]
    moved, _ = head_cols(flag_ref, hd)
    for slot, source in enumerate((own_ref, other_ref)):
        for g in range(2):
            at = pl.ds((2 * g + slot) * rows, rows)
            ch[at], cm[at] = parts2(source[g])
    ga_ref[...] = mul3((ch[...], cm[...]), parts2(wo_ref[...]), NT)
    for g, (a_ref, b_ref) in enumerate(((low_ref, first_ref), (last_ref, high_ref))):
        rim = jnp.concatenate([a_ref[...], b_ref[...]], axis=0)
        at = pl.ds(g * half, half)
        gq, gkv = group_back(q_ref[at, moved], rim, pm_ref[g], ga_ref[at, moved], scale)
        dq_ref[at] = gq
        if g == 0:
            left_ref[...] = gkv[:half]
            keep_ref[:half] = gkv[half:]
        else:
            keep_ref[half:] = gkv[:half]
            right_ref[...] = gkv[half:]


def still_back_kernel(scale, flag_ref, ga_ref, q_ref, kv_ref, ps_ref, dqm_ref, wq_ref, wk_ref, wv_ref, terms_ref, both):
    hd = dqm_ref.shape[1]
    moved, still = head_cols(flag_ref, hd)
    gq, gkv = group_back(q_ref[:, still], kv_ref[...], ps_ref[...], ga_ref[:, still], scale)
    both[:, moved] = dqm_ref[...]
    both[:, still] = gq
    terms_ref[...] = mul3(parts2(both[...]), parts2(wq_ref[...]), NT) + mul3(parts2(gkv), parts2(cat(wk_ref[:, still], wv_ref[:, still])), NT)


def finish_kernel(flag_ref, terms_ref, keep_ref, left_ref, right_ref, wk_ref, wv_ref, mine_ref, theirs_ref):
    moved, _ = head_cols(flag_ref, wk_ref.shape[1] // 2)
    rows = mine_ref.shape[1]
    grads = keep_ref[...] + jnp.concatenate([left_ref[...], right_ref[...]], axis=0)
    out = terms_ref[...] + mul3(parts2(grads), parts2(cat(wk_ref[:, moved], wv_ref[:, moved])), NT)
    for h in range(2):
        mine_ref[h] = out[2 * h * rows : (2 * h + 1) * rows]
        theirs_ref[h] = out[(2 * h + 1) * rows : (2 * h + 2) * rows]


def call(kernel, name, shapes, flag, *operands, scratch=(), flops=0):
    vmem = pl.BlockSpec(memory_space=pltpu.VMEM)
    out = [jax.ShapeDtypeStruct(s, F32) for s in shapes]
    size = sum(4 * math.prod(s) for s in shapes) + sum(4 * x.size for x in operands)
    return pl.pallas_call(
        kernel,
        out_shape=out,
        in_specs=[pl.BlockSpec(memory_space=pltpu.SMEM)] + [vmem] * len(operands),
        out_specs=[vmem] * len(shapes),
        scratch_shapes=list(scratch),
        compiler_params=pltpu.CompilerParams(vmem_limit_bytes=LIMIT),
        cost_estimate=pl.CostEstimate(flops=int(flops), bytes_accessed=size, transcendentals=0),
        name=name,
    )(flag, *operands)


LIMIT = 30 << 20


def rim_call(flag, own, other, gain, wk, wv):
    D, W = wk.shape
    T = 4 * own.shape[1]
    return call(rim_kernel, "rim_forward", [(T // 2, W)] * 2, flag, own, other, gain, wk, wv,
                scratch=[pltpu.VMEM((T, D), BF16)] * 3, flops=2 * T * D * W * 6)


def still_call(scale, flag, own, other, gain, wq, wk, wv):
    D, W = wk.shape
    T = 4 * own.shape[1]
    hd = W // 2
    return call(functools.partial(still_kernel, scale), "still_forward", [(T, W)] * 2 + [(T, T), (T, hd)], flag, own, other, gain, wq, wk, wv,
                scratch=[pltpu.VMEM((T, D), BF16)] * 3, flops=2 * T * D * hd * 24 + 2 * T * T * hd * 9)


def moved_call(scale, flag, q, first, last, low, high, out_still, wo):
    T, hd = out_still.shape
    D = wo.shape[1]
    return call(functools.partial(moved_kernel, scale), "moved_forward", [(2, T // 2, T), (2, T // 4, D), (2, T // 4, D)],
                flag, q, first, last, low, high, out_still, wo, scratch=[pltpu.VMEM((T, 2 * hd), F32)], flops=2 * T * D * hd * 6 + 2 * T * T * hd * 9)


def moved_back_call(scale, flag, own, other, wo, q, first, last, low, high, pm):
    T, hd = q.shape[0], q.shape[1] // 2
    D = wo.shape[1]
    return call(functools.partial(moved_back_kernel, scale), "moved_backward",
                [(T, 2 * hd), (T, hd), (T // 2, 2 * hd), (T // 2, 2 * hd), (T, 2 * hd)],
                flag, own, other, wo, q, first, last, low, high, pm,
                scratch=[pltpu.VMEM((T, D), BF16)] * 2, flops=2 * T * D * hd * 6 + 2 * T * T * hd * 12)


def still_back_call(scale, flag, ga, q, kv, ps, dqm, wq, wk, wv):
    T, hd = dqm.shape
    D = wq.shape[0]
    return call(functools.partial(still_back_kernel, scale), "still_backward", [(T, D)], flag, ga, q, kv, ps, dqm, wq, wk, wv,
                scratch=[pltpu.VMEM((T, 2 * hd), F32)], flops=2 * T * D * hd * 12 + 2 * T * T * hd * 12)[0]


def finish_call(flag, terms, keep, left, right, wk, wv):
    T, D = terms.shape
    return call(finish_kernel, "finish", [(2, T // 4, D)] * 2, flag, terms, keep, left, right, wk, wv, flops=2 * T * D * wk.shape[1] * 3)


CHIP = 2


def core_swap(x):
    length = lax.axis_size("head")
    return lax.ppermute(x, "head", [(i, i ^ 1) for i in range(length)])


def same_core():
    length = lax.axis_size("head")
    return [list(range(core, length, CHIP)) for core in range(CHIP)]


def gather_chips(rows):
    groups = same_core()
    chips = len(groups[0])
    sent = jnp.broadcast_to(rows[None], (chips,) + rows.shape)
    own = lax.all_to_all(sent, "head", 0, 0, tiled=True, axis_index_groups=groups)
    return own.reshape(2, -1, rows.shape[1])


def sum_chips(part):
    groups = same_core()
    chips = len(groups[0])
    split = part.reshape(chips, -1, part.shape[2])
    swapped = lax.all_to_all(split, "head", 0, 0, tiled=True, axis_index_groups=groups)
    return jnp.sum(swapped, axis=0)


def along(x, by):
    length = lax.axis_size("ctx")
    return lax.ppermute(x, "ctx", [(i, (i + by) % length) for i in range(length)])


def local(tokens, norm_gain, w_query, w_key, w_value, w_out, shift_heads, cotangent):
    scale = 1.0 / math.sqrt(w_query.shape[1] // 2)
    flag = shift_heads[1:2]
    gain = norm_gain[None]
    own = gather_chips(tokens)
    own, cot_later = lax.optimization_barrier((own, cotangent))
    other = core_swap(own)
    cot_own = gather_chips(cot_later)
    first, last = rim_call(flag, own, other, gain, w_key, w_value)
    low, high = along(last, 1), along(first, -1)
    query, kv_still, probs_still, out_still = still_call(scale, flag, own, other, gain, w_query, w_key, w_value)
    probs_moved, mine, theirs = moved_call(scale, flag, query, first, last, low, high, out_still, w_out)
    out_part = mine + core_swap(theirs)
    cot_own, out_part = lax.optimization_barrier((cot_own, out_part))
    out_sum = sum_chips(out_part)
    cot_other = core_swap(cot_own)
    grad_attention, grad_query, left, right, keep = moved_back_call(
        scale, flag, cot_own, cot_other, w_out, query, first, last, low, high, probs_moved
    )
    from_left, from_right = along(right, 1), along(left, -1)
    terms = still_back_call(
        scale, flag, grad_attention, query, kv_still, probs_still, grad_query, w_query, w_key, w_value
    )
    mine, theirs = finish_call(flag, terms, keep, from_left, from_right, w_key, w_value)
    grad_sum = sum_chips(mine + core_swap(theirs))
    mixed = tokens + out_sum
    inverse = lax.rsqrt(jnp.mean(tokens * tokens, axis=-1, keepdims=True) + 1e-06)
    weighted = grad_sum * norm_gain
    correction = jnp.mean(weighted * tokens, axis=-1, keepdims=True)
    input_grad = (
        cotangent + weighted * inverse - tokens * (inverse * inverse * inverse) * correction
    )
    return (mixed, input_grad)


def solution(mesh):
    placed = (
        P(("ctx", "head"), None),
        P(),
        P(None, "head"),
        P(None, "head"),
        P(None, "head"),
        P("head", None),
        P("head"),
        P(("ctx", "head"), None),
    )
    return jax.shard_map(
        local,
        mesh=mesh,
        in_specs=placed,
        out_specs=(P(("ctx", "head"), None), P(("ctx", "head"), None)),
        check_vma=False,
    )
```

time: 511 us -> 183 us (0.36); the launches traced: 502 us -> 181 us
  waiting for transfers between devices: 390 us -> 50.8 us
  matrix products: 47.4 us -> 0 us
  blocking collectives: 0 us -> 39.4 us
  starting transfers between devices: 13 us -> 45.7 us
  Pallas kernels: 6.87 us -> 25.7 us
  between operations: 15.3 us -> 1 us
  other arithmetic: 14.5 us -> 4.46 us
    reduce_scatter x2 -> x0, waiting for transfers between devices: 242 us -> none  [the longest x1 122 us: local(): lax.psum_scatter(out_terms, 'head', scatter_dimension=0, tiled=True)]
    all_gather x2 -> x0, waiting for transfers between devices: 136 us -> none  [the longest x1 71.7 us: local(): cot_rows = lax.all_gather(cotangent, 'head', axis=0, tiled=True)]
    dot_general x18 -> x0, matrix products: 47.4 us -> none  [the longest x1 5.92 us: local(): jnp.dot(join_heads(grad_query_moved, grad_query_still[0]), w_query.T, pre...]
    all_to_all x0 -> x1, blocking collectives: none -> 39.4 us  [gather_chips(): lax.all_to_all(sent, 'head', 0, 0, tiled=True, axis_index_groups=groups)]
    all_to_all x0 -> x3, waiting for transfers between devices: none -> 26.6 us  [the longest x2 26.6 us: sum_chips(): lax.all_to_all(split, 'head', 0, 0, tiled=True, axis_index_groups=groups)]
    pallas_call x0 -> x6, Pallas kernels: none -> 25.7 us  [call(): pl.pallas_call(kernel, out_shape=out, in_specs=[pl.BlockSpec(memory_space...]
    all_to_all x0 -> x3, starting transfers between devices: none -> 21.6 us  [the longest x2 18 us: sum_chips(): lax.all_to_all(split, 'head', 0, 0, tiled=True, axis_index_groups=groups)]
    ppermute x4 -> x8, waiting for transfers between devices: 10.3 us -> 24.2 us  [the longest x4 19 us: along(): lax.ppermute(x, 'ctx', [(i, (i + by) % length) for i in range(length)])]
  transfers between devices with their start and end apart: 8 -> 11, of which waited for: 6 -> 6; matrix products, arithmetic and copies ran while one was open for 5% -> 3% of each run, Pallas kernels for 1% -> 14%
where the time goes in v1:
time: 183 us; the launch traced here: 181 us
  waiting for transfers between devices  50.8 us (28%)
  starting transfers between devices  45.7 us (25%)
  blocking collectives  39.4 us (22%)
  Pallas kernels  25.7 us (14%)
  local copies, waits for them, and re-layouts  13.5 us (7%)
  other arithmetic  4.46 us (2%)
    all_to_all x1, blocking collectives, gather_chips(): lax.all_to_all(sent, 'head', 0, 0, tiled=True, axis_index_groups=groups)  39.4 us
    all_to_all x2, waiting for transfers between devices, sum_chips(): lax.all_to_all(split, 'head', 0, 0, tiled=True, axis_index_groups=groups)  26.6 us
    pallas_call x6, Pallas kernels, call(): pl.pallas_call(kernel, out_shape=out, in_specs=[pl.BlockSpec(memory_space...  25.7 us
    ppermute x4, waiting for transfers between devices, along(): lax.ppermute(x, 'ctx', [(i, (i + by) % length) for i in range(length)])  19 us
    all_to_all x2, starting transfers between devices, sum_chips(): lax.all_to_all(split, 'head', 0, 0, tiled=True, axis_index_groups=groups)  18 us
    ppermute x4, starting transfers between devices, along(): lax.ppermute(x, 'ctx', [(i, (i + by) % length) for i in range(length)])  16.2 us
    unnamed x54, local copies, waits for them, and re-layouts  10.8 us
    ppermute x4, starting transfers between devices, core_swap(): return lax.ppermute(x, 'head', [(i, i ^ 1) for i in range(length)])  7.9 us
  transfers between devices with their start and end apart: 11, of which 6 were waited for; matrix products, arithmetic and copies ran while one was open for 3% of the time, Pallas kernels for 14%

profile of v1, /device:TPU:6, one launch (start us, length us, event | category | flops | bytes accessed | tf_op | source)
XLA Modules:
  0.0 180.7 jit_solution(7506601069052779420)
XLA Ops:
  0.6 1.0 broadcast_in_dim.6
  1.6 39.4 %all_to_all.20 = f32[16,16,1024]{2,1,0:T(8,128)S(1)} all-to-all(f32[16,16,1024]{2,1,0:T(8,128)S(1)} %broadcast_in_dim.6), channel_id=1, replica_groups={{0,2,4,6,8,10,12,14,16,18,20,22,24,26,28,30},{1,3,5,7,9,11,13,15,17,19,..., dimensions={0} | all-to-all | bytes 2097152 | tf_op jit(solution)/shard_map/all_to_all | solution.py:260
  41.1 2.0 %collective-permute-start = (f32[2,128,1024]{2,1,0:T(8,128)S(1)}, f32[2,128,1024]{2,1,0:T(8,128)}, u32[]{:S(2)}, u32[]{:S(2)}) collective-permute-start(f32[2,128,1024]{2,1,0:T(8,128)S(1)} %bitcast.7), channel_id=1, source_target_pairs={{0,1},{1,0},{2,3},{3,2},{4,5},{5,4},{6,7},{7,6},{8,9},{9,8},{10,11... | collective-permute-start | bytes 3145736 | tf_op jit(solution)/shard_map/ppermute | solution.py:248
  43.1 1.1 broadcast_in_dim.7
  44.2 3.7 %all-to-all-start.1 = ((f32[16,16,1024]{2,1,0:T(8,128)}), f32[16,16,1024]{2,1,0:T(8,128)S(1)}, u32[]{:S(2)}, u32[]{:S(2)}) async-start(f32[16,16,1024]{2,1,0:T(8,128)} %broadcast_in_dim.7), calls=%async_computation.1 | async-start | bytes 2097152 | tf_op jit(solution)/shard_map/all_to_all | solution.py:260
  47.9 0.6 slice.3.flag_ref
  48.5 0.0 collective-permute-done.other_ref
  48.5 0.0 copy-start.1
  48.5 1.2 copy-done.1
  49.7 4.8 %rim_forward.1 = (f32[256,256]{1,0:T(8,128)S(1)}, f32[256,256]{1,0:T(8,128)S(1)}) custom-call(s32[1]{0:T(128)} %slice.3.flag_ref, f32[2,128,1024]{2,1,0:T(8,128)S(1)} %bitcast.8, f32[2,128,1024]{2,1,0:T(8,128)} %collective-permute-done.other_ref, f32[1,1024]{1,0:T(1,128)S(1)} %bitcast.10, f32[1024,256]{1,0:T(8,128)S(1)} %copy-done, f32[1024,256]{1,0:T(8,128)S(1)} %copy-done.1), custom_call_target="tpu_custom_call" | custom-call | flops 1610612736 | bytes 4722688 | tf_op jit(solution)/shard_map/rim_forward/pallas_call | solution.py:185
  54.6 2.7 %collective-permute-start.2 = (f32[256,256]{1,0:T(8,128)S(1)}, f32[256,256]{1,0:T(8,128)S(1)}, u32[]{:S(2)}, u32[]{:S(2)}) collective-permute-start(f32[256,256]{1,0:T(8,128)S(1)} %get-tuple-element.25.first_ref), channel_id=1, source_target_pairs={{0,480},{32,0},{64,32},{96,64},{128,96},{160,128},{192,160},{224,1... | collective-permute-start | bytes 786440 | tf_op jit(solution)/shard_map/ppermute | solution.py:274
  57.3 0.0 copy-start.4
  57.3 6.2 %collective-permute-start.1 = (f32[256,256]{1,0:T(8,128)S(1)}, f32[256,256]{1,0:T(8,128)S(1)}, u32[]{:S(2)}, u32[]{:S(2)}) collective-permute-start(f32[256,256]{1,0:T(8,128)S(1)} %get-tuple-element.26.last_ref), channel_id=1, source_target_pairs={{0,32},{32,64},{64,96},{96,128},{128,160},{160,192},{192,224},{224... | collective-permute-start | bytes 786440 | tf_op jit(solution)/shard_map/ppermute | solution.py:274
  63.6 7.6 %still_forward.1 = (f32[512,256]{1,0:T(8,128)S(1)}, f32[512,256]{1,0:T(8,128)S(1)}, f32[512,512]{1,0:T(8,128)S(1)}, f32[512,128]{1,0:T(8,128)S(1)}) custom-call(s32[1]{0:T(128)} %slice.3.flag_ref, f32[2,128,1024]{2,1,0:T(8,128)S(1)} %bitcast.9, f32[2,128,1024]{2,1,0:T(8,128)} %collective-permute-done.other_ref, f32[1,1024]{1,0:T(1,128)S(1)} %bitcast.11, ...), custom_call_target="tpu_custom_call" | custom-call | flops 3825205248 | bytes 7606272 | tf_op jit(solution)/shard_map/still_forward/pallas_call | solution.py:185
  71.2 8.1 %collective-permute-done.1.low_ref = f32[256,256]{1,0:T(8,128)S(1)} collective-permute-done((f32[256,256]{1,0:T(8,128)S(1)}, f32[256,256]{1,0:T(8,128)S(1)}, u32[]{:S(2)}, u32[]{:S(2)}) %collective-permute-start.1) | collective-permute-done | bytes 262176 | tf_op jit(solution)/shard_map/ppermute | solution.py:274
  79.4 3.2 %moved_forward.1 = (f32[2,256,512]{2,1,0:T(8,128)S(1)}, f32[2,128,1024]{2,1,0:T(8,128)S(1)}, f32[2,128,1024]{2,1,0:T(8,128)S(1)}) custom-call(s32[1]{0:T(128)} %slice.3.flag_ref, f32[512,256]{1,0:T(8,128)S(1)} %get-tuple-element.24.q_ref, f32[256,256]{1,0:T(8,128)S(1)} %get-tuple-element.25.first_ref, f32[256,256]{1,0:T(8,128)S(1)} %get-tuple-element.26.last_ref, ...), custom_call_target="tpu_custom_call" | custom-call | flops 1409286144 | bytes 6029312 | tf_op jit(solution)/shard_map/moved_forward/pallas_call | solution.py:185
  82.6 1.0 copy-done.16
  83.6 1.9 %collective-permute-start.3 = (f32[2,128,1024]{2,1,0:T(8,128)S(1)}, f32[2,128,1024]{2,1,0:T(8,128)S(1)}, u32[]{:S(2)}, u32[]{:S(2)}) collective-permute-start(f32[2,128,1024]{2,1,0:T(8,128)S(1)} %get-tuple-element.29), channel_id=1, source_target_pairs={{0,1},{1,0},{2,3},{3,2},{4,5},{5,4},{6,7},{7,6},{8,9},{9,8},{10,11... | collective-permute-start | bytes 3145736 | tf_op jit(solution)/shard_map/ppermute | solution.py:248
  85.5 2.6 %collective-permute-done.3 = f32[2,128,1024]{2,1,0:T(8,128)S(1)} collective-permute-done((f32[2,128,1024]{2,1,0:T(8,128)S(1)}, f32[2,128,1024]{2,1,0:T(8,128)S(1)}, u32[]{:S(2)}, u32[]{:S(2)}) %collective-permute-start.3) | collective-permute-done | bytes 1048608 | tf_op jit(solution)/shard_map/ppermute | solution.py:248
  88.1 1.1 add.23
  89.2 0.0 all-to-all-done.1
  89.2 2.0 %collective-permute-start.4 = (f32[2,128,1024]{2,1,0:T(8,128)S(1)}, f32[2,128,1024]{2,1,0:T(8,128)S(1)}, u32[]{:S(2)}, u32[]{:S(2)}) collective-permute-start(f32[2,128,1024]{2,1,0:T(8,128)S(1)} %bitcast.5), channel_id=1, source_target_pairs={{0,1},{1,0},{2,3},{3,2},{4,5},{5,4},{6,7},{7,6},{8,9},{9,8},{10,11... | collective-permute-start | bytes 3145736 | tf_op jit(solution)/shard_map/ppermute | solution.py:248
  91.3 8.9 %all-to-all-start.2 = ((f32[16,16,1024]{2,1,0:T(8,128)}), f32[16,16,1024]{2,1,0:T(8,128)}, u32[]{:S(2)}, u32[]{:S(2)}) async-start(f32[16,16,1024]{2,1,0:T(8,128)} %bitcast.12), calls=%async_computation.2 | async-start | bytes 2097152 | tf_op jit(solution)/shard_map/all_to_all | solution.py:268
  100.2 0.0 collective-permute-done.4.other_ref
  100.2 1.0 copy-done.8
  101.2 1.2 copy-done.5
  102.5 1.2 copy-done.9
  103.7 0.9 copy-done.11
  104.6 0.9 copy-done.13
  105.6 0.9 copy-done.15
  106.5 1.2 copy-done.17
  107.8 1.0 copy-done.19
  108.8 4.7 %moved_backward.1 = (f32[512,256]{1,0:T(8,128)S(1)}, f32[512,128]{1,0:T(8,128)S(1)}, f32[256,256]{1,0:T(8,128)S(1)}, f32[256,256]{1,0:T(8,128)S(1)}, f32[512,256]{1,0:T(8,128)S(1)}) custom-call(s32[1]{0:T(128)} %slice.3.flag_ref, f32[2,128,1024]{2,1,0:T(8,128)S(1)} %bitcast.6, f32[2,128,1024]{2,1,0:T(8,128)S(1)} %copy-done.9, f32[256,1024]{1,0:T(8,128)S(1)} %copy-done.5, ...), custom_call_target="tpu_custom_call" | custom-call | flops 1610612736 | bytes 7602176 | tf_op jit(solution)/shard_map/moved_backward/pallas_call | solution.py:185
  113.6 5.3 %collective-permute-start.5 = (f32[256,256]{1,0:T(8,128)S(1)}, f32[256,256]{1,0:T(8,128)S(1)}, u32[]{:S(2)}, u32[]{:S(2)}) collective-permute-start(f32[256,256]{1,0:T(8,128)S(1)} %get-tuple-element.38), channel_id=1, source_target_pairs={{0,32},{32,64},{64,96},{96,128},{128,160},{160,192},{192,224},{224... | collective-permute-start | bytes 786440 | tf_op jit(solution)/shard_map/ppermute | solution.py:274
  118.9 1.9 %collective-permute-start.6 = (f32[256,256]{1,0:T(8,128)S(1)}, f32[256,256]{1,0:T(8,128)S(1)}, u32[]{:S(2)}, u32[]{:S(2)}) collective-permute-start(f32[256,256]{1,0:T(8,128)S(1)} %get-tuple-element.39), channel_id=1, source_target_pairs={{0,480},{32,0},{64,32},{96,64},{128,96},{160,128},{192,160},{224,1... | collective-permute-start | bytes 786440 | tf_op jit(solution)/shard_map/ppermute | solution.py:274
  120.9 3.8 %still_backward.1.terms_ref = f32[512,1024]{1,0:T(8,128)S(1)} custom-call(s32[1]{0:T(128)} %slice.3.flag_ref, f32[512,256]{1,0:T(8,128)S(1)} %get-tuple-element.33.ga_ref, f32[512,256]{1,0:T(8,128)S(1)} %copy-done.19, f32[512,256]{1,0:T(8,128)S(1)} %copy-done.23, f32[512,512]{1,0:T(8,128)S(1)} %copy-done.21, f32[512,128]{1,0:T(8,128)S(1)} %get-tuple-element.36.dqm_ref, ...), custom_call_target="tpu_custom_call" | custom-call | flops 2415919104 | bytes 8126464 | tf_op jit(solution)/shard_map/still_backward/pallas_call | solution.py:185
  124.6 2.2 %collective-permute-done.5.left_ref = f32[256,256]{1,0:T(8,128)S(1)} collective-permute-done((f32[256,256]{1,0:T(8,128)S(1)}, f32[256,256]{1,0:T(8,128)S(1)}, u32[]{:S(2)}, u32[]{:S(2)}) %collective-permute-start.5) | collective-permute-done | bytes 262176 | tf_op jit(solution)/shard_map/ppermute | solution.py:274
  126.8 8.7 %collective-permute-done.6.right_ref = f32[256,256]{1,0:T(8,128)S(1)} collective-permute-done((f32[256,256]{1,0:T(8,128)S(1)}, f32[256,256]{1,0:T(8,128)S(1)}, u32[]{:S(2)}, u32[]{:S(2)}) %collective-permute-start.6) | collective-permute-done | bytes 262176 | tf_op jit(solution)/shard_map/ppermute | solution.py:274
  135.4 1.7 finish.1
  137.1 1.9 %collective-permute-start.7 = (f32[2,128,1024]{2,1,0:T(8,128)S(1)}, f32[2,128,1024]{2,1,0:T(8,128)S(1)}, u32[]{:S(2)}, u32[]{:S(2)}) collective-permute-start(f32[2,128,1024]{2,1,0:T(8,128)S(1)} %get-tuple-element.41), channel_id=1, source_target_pairs={{0,1},{1,0},{2,3},{3,2},{4,5},{5,4},{6,7},{7,6},{8,9},{9,8},{10,11... | collective-permute-start | bytes 3145736 | tf_op jit(solution)/shard_map/ppermute | solution.py:248
  139.1 2.6 %collective-permute-done.7 = f32[2,128,1024]{2,1,0:T(8,128)S(1)} collective-permute-done((f32[2,128,1024]{2,1,0:T(8,128)S(1)}, f32[2,128,1024]{2,1,0:T(8,128)S(1)}, u32[]{:S(2)}, u32[]{:S(2)}) %collective-permute-start.7) | collective-permute-done | bytes 1048608 | tf_op jit(solution)/shard_map/ppermute | solution.py:248
  141.7 1.2 add.25
  142.8 9.1 %all-to-all-start.3 = ((f32[16,16,1024]{2,1,0:T(8,128)}), f32[16,16,1024]{2,1,0:T(8,128)S(1)}, u32[]{:S(2)}, u32[]{:S(2)}) async-start(f32[16,16,1024]{2,1,0:T(8,128)} %bitcast.4), calls=%async_computation.3 | async-start | bytes 2097152 | tf_op jit(solution)/shard_map/all_to_all | solution.py:268
  151.9 1.3 reduce_sum.36
  153.2 26.6 %all-to-all-done.3 = f32[16,16,1024]{2,1,0:T(8,128)S(1)} async-done(((f32[16,16,1024]{2,1,0:T(8,128)}), f32[16,16,1024]{2,1,0:T(8,128)S(1)}, u32[]{:S(2)}, u32[]{:S(2)}) %all-to-all-start.3) | async-done | bytes 1048608 | tf_op jit(solution)/shard_map/all_to_all | solution.py:268
  179.8 0.1 reduce_sum.37
  179.8 0.1 multiply_reduce_fusion.1
  180.0 0.7 multiply_subtract_fusion
  (45 shorter events, 0.1 us)
Async XLA Ops:
  0.6 42.5 %copy-start.25 = (f32[16,1024]{1,0:T(8,128)S(1)}, f32[16,1024]{1,0:T(8,128)}, u32[]{:S(2)}) copy-start(f32[16,1024]{1,0:T(8,128)} %param.15) | copy-start | bytes 196612
  41.1 6.8 %copy-start.26 = (s32[2]{0:T(128)S(1)}, s32[2]{0:T(128)}, u32[]{:S(2)}) copy-start(s32[2]{0:T(128)} %param.14) | copy-start | bytes 28
  41.1 7.4 %copy-start = (f32[1024,256]{1,0:T(8,128)S(1)}, f32[1024,256]{1,0:T(8,128)}, u32[]{:S(2)}) copy-start(f32[1024,256]{1,0:T(8,128)} %wk_ref.7) | copy-start | bytes 3145732
  41.1 7.4 %copy-start.3 = (f32[1024]{0:T(1024)S(1)}, f32[1024]{0:T(1024)}, u32[]{:S(2)}) copy-start(f32[1024]{0:T(1024)} %param.9) | copy-start | bytes 12292
  41.1 7.4 %collective-permute-start = (f32[2,128,1024]{2,1,0:T(8,128)S(1)}, f32[2,128,1024]{2,1,0:T(8,128)}, u32[]{:S(2)}, u32[]{:S(2)}) collective-permute-start(f32[2,128,1024]{2,1,0:T(8,128)S(1)} %bitcast.7), channel_id=1, source_target_pairs={{0,1},{1,0},{2,3},{3,2},{4,5},{5,4},{6,7},{7,6},{8,9},{9,8},{10,11... | collective-permute-start | bytes 3145736 | tf_op jit(solution)/shard_map/ppermute | solution.py:248
  44.2 45.0 %all-to-all-start.1 = ((f32[16,16,1024]{2,1,0:T(8,128)}), f32[16,16,1024]{2,1,0:T(8,128)S(1)}, u32[]{:S(2)}, u32[]{:S(2)}) async-start(f32[16,16,1024]{2,1,0:T(8,128)} %broadcast_in_dim.7), calls=%async_computation.1 | async-start | bytes 2097152 | tf_op jit(solution)/shard_map/all_to_all | solution.py:260
  48.5 1.2 copy-start.1
  49.7 13.9 %copy-start.6 = (f32[1024,256]{1,0:T(8,128)S(1)}, f32[1024,256]{1,0:T(8,128)}, u32[]{:S(2)}) copy-start(f32[1024,256]{1,0:T(8,128)} %wq_ref.3) | copy-start | bytes 3145732
  54.6 24.8 %copy-start.10 = (f32[256,256]{1,0:T(8,128)}, f32[256,256]{1,0:T(8,128)S(1)}, u32[]{:S(2)}) copy-start(f32[256,256]{1,0:T(8,128)S(1)} %get-tuple-element.26.last_ref) | copy-start | bytes 786436
  54.6 16.6 %collective-permute-start.2 = (f32[256,256]{1,0:T(8,128)S(1)}, f32[256,256]{1,0:T(8,128)S(1)}, u32[]{:S(2)}, u32[]{:S(2)}) collective-permute-start(f32[256,256]{1,0:T(8,128)S(1)} %get-tuple-element.25.first_ref), channel_id=1, source_target_pairs={{0,480},{32,0},{64,32},{96,64},{128,96},{160,128},{192,160},{224,1... | collective-permute-start | bytes 786440 | tf_op jit(solution)/shard_map/ppermute | solution.py:274
  57.3 22.0 %copy-start.4 = (f32[256,1024]{1,0:T(8,128)S(1)}, f32[256,1024]{1,0:T(8,128)}, u32[]{:S(2)}) copy-start(f32[256,1024]{1,0:T(8,128)} %wo_ref.3) | copy-start | bytes 3145732
  57.3 22.0 %collective-permute-start.1 = (f32[256,256]{1,0:T(8,128)S(1)}, f32[256,256]{1,0:T(8,128)S(1)}, u32[]{:S(2)}, u32[]{:S(2)}) collective-permute-start(f32[256,256]{1,0:T(8,128)S(1)} %get-tuple-element.26.last_ref), channel_id=1, source_target_pairs={{0,32},{32,64},{64,96},{96,128},{128,160},{160,192},{192,224},{224... | collective-permute-start | bytes 786440 | tf_op jit(solution)/shard_map/ppermute | solution.py:274
  71.2 11.4 %copy-start.18 = (f32[512,256]{1,0:T(8,128)}, f32[512,256]{1,0:T(8,128)S(1)}, u32[]{:S(2)}) copy-start(f32[512,256]{1,0:T(8,128)S(1)} %get-tuple-element.24.q_ref) | copy-start | bytes 1572868
  71.2 11.4 %copy-start.20 = (f32[512,512]{1,0:T(8,128)}, f32[512,512]{1,0:T(8,128)S(1)}, u32[]{:S(2)}) copy-start(f32[512,512]{1,0:T(8,128)S(1)} %get-tuple-element.35.ps_ref) | copy-start | bytes 3145732
  71.2 11.4 %copy-start.22 = (f32[512,256]{1,0:T(8,128)}, f32[512,256]{1,0:T(8,128)S(1)}, u32[]{:S(2)}) copy-start(f32[512,256]{1,0:T(8,128)S(1)} %get-tuple-element.34.kv_ref) | copy-start | bytes 1572868
  71.2 11.4 %copy-start.12 = (f32[256,256]{1,0:T(8,128)}, f32[256,256]{1,0:T(8,128)S(1)}, u32[]{:S(2)}) copy-start(f32[256,256]{1,0:T(8,128)S(1)} %collective-permute-done.2.high_ref) | copy-start | bytes 786436
  79.4 3.2 %copy-start.14 = (f32[256,256]{1,0:T(8,128)}, f32[256,256]{1,0:T(8,128)S(1)}, u32[]{:S(2)}) copy-start(f32[256,256]{1,0:T(8,128)S(1)} %collective-permute-done.1.low_ref) | copy-start | bytes 786436
  82.6 1.0 copy-start.16
  83.6 4.5 %collective-permute-start.3 = (f32[2,128,1024]{2,1,0:T(8,128)S(1)}, f32[2,128,1024]{2,1,0:T(8,128)S(1)}, u32[]{:S(2)}, u32[]{:S(2)}) collective-permute-start(f32[2,128,1024]{2,1,0:T(8,128)S(1)} %get-tuple-element.29), channel_id=1, source_target_pairs={{0,1},{1,0},{2,3},{3,2},{4,5},{5,4},{6,7},{7,6},{8,9},{9,8},{10,11... | collective-permute-start | bytes 3145736 | tf_op jit(solution)/shard_map/ppermute | solution.py:248
  89.2 11.0 %collective-permute-start.4 = (f32[2,128,1024]{2,1,0:T(8,128)S(1)}, f32[2,128,1024]{2,1,0:T(8,128)S(1)}, u32[]{:S(2)}, u32[]{:S(2)}) collective-permute-start(f32[2,128,1024]{2,1,0:T(8,128)S(1)} %bitcast.5), channel_id=1, source_target_pairs={{0,1},{1,0},{2,3},{3,2},{4,5},{5,4},{6,7},{7,6},{8,9},{9,8},{10,11... | collective-permute-start | bytes 3145736 | tf_op jit(solution)/shard_map/ppermute | solution.py:248
  91.3 51.6 %all-to-all-start.2 = ((f32[16,16,1024]{2,1,0:T(8,128)}), f32[16,16,1024]{2,1,0:T(8,128)}, u32[]{:S(2)}, u32[]{:S(2)}) async-start(f32[16,16,1024]{2,1,0:T(8,128)} %bitcast.12), calls=%async_computation.2 | async-start | bytes 2097152 | tf_op jit(solution)/shard_map/all_to_all | solution.py:268
  100.2 1.0 copy-start.8
  101.2 1.2 copy-start.5
  102.5 1.2 copy-start.9
  103.7 0.9 copy-start.11
  104.6 0.9 copy-start.13
  105.6 0.9 copy-start.15
  106.5 1.2 copy-start.17
  107.8 1.0 copy-start.19
  108.8 12.0 %copy-start.2 = (f32[1024,256]{1,0:T(8,128)S(1)}, f32[1024,256]{1,0:T(8,128)}, u32[]{:S(2)}) copy-start(f32[1024,256]{1,0:T(8,128)} %wv_ref.7) | copy-start | bytes 3145732
  108.8 12.0 %copy-start.7 = (f32[1024,256]{1,0:T(8,128)S(1)}, f32[1024,256]{1,0:T(8,128)}, u32[]{:S(2)}) copy-start(f32[1024,256]{1,0:T(8,128)} %wq_ref.3) | copy-start | bytes 3145732
  108.8 12.0 %copy-start.21 = (f32[512,512]{1,0:T(8,128)S(1)}, f32[512,512]{1,0:T(8,128)}, u32[]{:S(2)}) copy-start(f32[512,512]{1,0:T(8,128)} %copy-done.20) | copy-start | bytes 3145732
  108.8 12.0 %copy-start.23 = (f32[512,256]{1,0:T(8,128)S(1)}, f32[512,256]{1,0:T(8,128)}, u32[]{:S(2)}) copy-start(f32[512,256]{1,0:T(8,128)} %copy-done.22) | copy-start | bytes 1572868
  113.6 13.2 %collective-permute-start.5 = (f32[256,256]{1,0:T(8,128)S(1)}, f32[256,256]{1,0:T(8,128)S(1)}, u32[]{:S(2)}, u32[]{:S(2)}) collective-permute-start(f32[256,256]{1,0:T(8,128)S(1)} %get-tuple-element.38), channel_id=1, source_target_pairs={{0,32},{32,64},{64,96},{96,128},{128,160},{160,192},{192,224},{224... | collective-permute-start | bytes 786440 | tf_op jit(solution)/shard_map/ppermute | solution.py:274
  118.9 16.6 %collective-permute-start.6 = (f32[256,256]{1,0:T(8,128)S(1)}, f32[256,256]{1,0:T(8,128)S(1)}, u32[]{:S(2)}, u32[]{:S(2)}) collective-permute-start(f32[256,256]{1,0:T(8,128)S(1)} %get-tuple-element.39), channel_id=1, source_target_pairs={{0,480},{32,0},{64,32},{96,64},{128,96},{160,128},{192,160},{224,1... | collective-permute-start | bytes 786440 | tf_op jit(solution)/shard_map/ppermute | solution.py:274
  137.1 4.6 %collective-permute-start.7 = (f32[2,128,1024]{2,1,0:T(8,128)S(1)}, f32[2,128,1024]{2,1,0:T(8,128)S(1)}, u32[]{:S(2)}, u32[]{:S(2)}) collective-permute-start(f32[2,128,1024]{2,1,0:T(8,128)S(1)} %get-tuple-element.41), channel_id=1, source_target_pairs={{0,1},{1,0},{2,3},{3,2},{4,5},{5,4},{6,7},{7,6},{8,9},{9,8},{10,11... | collective-permute-start | bytes 3145736 | tf_op jit(solution)/shard_map/ppermute | solution.py:248
  142.8 37.0 %copy-start.24 = (f32[16,1024]{1,0:T(8,128)S(1)}, f32[16,1024]{1,0:T(8,128)}, u32[]{:S(2)}) copy-start(f32[16,1024]{1,0:T(8,128)} %param.8) | copy-start | bytes 196612
  142.8 36.9 %all-to-all-start.3 = ((f32[16,16,1024]{2,1,0:T(8,128)}), f32[16,16,1024]{2,1,0:T(8,128)S(1)}, u32[]{:S(2)}, u32[]{:S(2)}) async-start(f32[16,16,1024]{2,1,0:T(8,128)} %bitcast.4), calls=%async_computation.3 | async-start | bytes 2097152 | tf_op jit(solution)/shard_map/all_to_all | solution.py:268

commit v2 on v1

v2 whole, which is shorter than its diff:
```python
import functools
import math

import jax
import jax.numpy as jnp
from jax import lax
from jax.experimental import pallas as pl
from jax.experimental.pallas import tpu as pltpu
from jax.sharding import PartitionSpec as P

F32, BF16 = jnp.float32, jnp.bfloat16
NN, NT, TN = ((1,), (0,)), ((1,), (1,)), ((0,), (0,))


def parts2(x):
    high = x.astype(BF16)
    return high, (x - high.astype(F32)).astype(BF16)


def parts3(x):
    high = x.astype(BF16)
    rest = x - high.astype(F32)
    middle = rest.astype(BF16)
    return high, middle, (rest - middle.astype(F32)).astype(BF16)


def mul(a, b, dims):
    return lax.dot_general(a, b, (dims, ((), ())), preferred_element_type=F32)


def mul3(a, b, dims):
    return mul(a[0], b[0], dims) + (mul(a[0], b[1], dims) + mul(a[1], b[0], dims))


def mul6(a, b, dims):
    small = mul(a[1], b[1], dims) + mul(a[0], b[2], dims) + mul(a[2], b[0], dims)
    return mul(a[0], b[0], dims) + (mul(a[0], b[1], dims) + mul(a[1], b[0], dims) + small)


def cat(a, b):
    return jnp.concatenate([a, b], axis=1)


def scores6(a, b):
    (ah, am, al), (bh, bm, bl) = a, b
    wide = cat(bh, bm)
    return mul(cat(ah, ah), wide, NT) + (mul(cat(am, am), wide, NT) + mul(cat(ah, al), cat(bl, bh), NT))


def scores3(a, b):
    (ah, am), (bh, bm) = a, b
    return mul(cat(ah, am), cat(bh, bh), NT) + mul(ah, bm, NT)


def weigh3(a, b, dims):
    width = b[0].shape[1]
    both = mul(a[0], cat(b[0], b[1]), dims)
    return both[:, :width] + (both[:, width:] + mul(a[1], b[0], dims))


def head_cols(flag_ref, width):
    second = flag_ref[0]
    moved = pl.multiple_of(second * width, width)
    still = pl.multiple_of((1 - second) * width, width)
    return pl.ds(moved, width), pl.ds(still, width)


def normed_parts(own, other, gain_ref, refs):
    for slot, source in enumerate((own, other)):
        rows = source.shape[1]

        @pl.loop(0, 2)
        def _(half):
            x = source[half]
            x = x * lax.rsqrt(jnp.mean(x * x, axis=-1, keepdims=True) + 1e-06) * gain_ref[...]
            at = pl.ds(pl.multiple_of((2 * half + slot) * rows, rows), rows)
            for ref, part in zip(refs, parts3(x)):
                ref[at] = part


def softmax_rows(scores):
    powers = jnp.exp(scores - jnp.max(scores, axis=-1, keepdims=True))
    return powers / jnp.sum(powers, axis=-1, keepdims=True)


def rim_kernel(flag_ref, own, wk, wv, other, gain_ref, first_ref, last_ref, nh, nm, nl):
    normed_parts(own, other, gain_ref, (nh, nm, nl))
    moved, _ = head_cols(flag_ref, wk.shape[1] // 2)
    half = first_ref.shape[0]
    both = mul6((nh[...], nm[...], nl[...]), parts3(cat(wk[:, moved], wv[:, moved])), NN)
    first_ref[...] = both[:half]
    last_ref[...] = both[half:]


def still_kernel(scale, flag_ref, wk, wv, wq, nh, nm, nl, qm_ref, qs_ref, kv_ref, ps_ref, os_ref, q_ref):
    hd = wk.shape[1] // 2
    moved, still = head_cols(flag_ref, hd)
    n = (nh[...], nm[...], nl[...])
    kv_ref[...] = mul6(n, parts3(cat(wk[:, still], wv[:, still])), NN)
    q_ref[...] = mul6(n, parts3(wq[...]), NN)
    qm_ref[...] = q_ref[:, moved]
    qs_ref[...] = q_ref[:, still]
    scores = scores6(parts3(qs_ref[...]), parts3(kv_ref[:, :hd])) * scale
    probs = softmax_rows(scores)
    ps_ref[...] = probs
    os_ref[...] = weigh3(parts2(probs), parts2(kv_ref[:, hd:]), NN)


def moved_kernel(scale, flag_ref, q_ref, first_ref, last_ref, wo, os_ref, low_ref, high_ref, pm_ref, mine_ref, theirs_ref, both):
    hd = os_ref.shape[1]
    half = first_ref.shape[0]
    moved, still = head_cols(flag_ref, hd)
    for g, (a_ref, b_ref) in enumerate(((low_ref, first_ref), (last_ref, high_ref))):
        rim = jnp.concatenate([a_ref[...], b_ref[...]], axis=0)
        at = pl.ds(g * half, half)
        scores = scores6(parts3(q_ref[at]), parts3(rim[:, :hd])) * scale
        probs = softmax_rows(scores)
        pm_ref[g] = probs
        both[at, moved] = weigh3(parts2(probs), parts2(rim[:, hd:]), NN)
    both[:, still] = os_ref[...]
    rows = mine_ref.shape[1]
    out = mul3(parts2(both[...]), parts2(wo[...]), NN)
    for g in range(2):
        mine_ref[g] = out[2 * g * rows : (2 * g + 1) * rows]
        theirs_ref[g] = out[(2 * g + 1) * rows : (2 * g + 2) * rows]


def group_back(query, kv, probs, grad_out, scale):
    hd = query.shape[1]
    q, k, v, g = parts2(query), parts2(kv[:, :hd]), parts2(kv[:, hd:]), parts2(grad_out)
    grad_probs = scores3(g, v)
    inner = jnp.sum(probs * grad_probs, axis=-1, keepdims=True)
    grad_values = weigh3(parts2(probs), g, TN)
    grad_scores = parts2(probs * (grad_probs - inner) * scale)
    grad_query = weigh3(grad_scores, k, NN)
    grad_keys = weigh3(grad_scores, q, TN)
    return grad_query, cat(grad_keys, grad_values)


def moved_back_kernel(scale, flag_ref, q, rim_low, rim_first, pm, rim_last, rim_high, own, other, wo, gs_ref, dq_ref, left_ref, right_ref, keep_ref, ch, cm, ga_ref):
    for slot, source in enumerate((own, other)):
        rows = source.shape[1]
        for g in range(2):
            at = pl.ds((2 * g + slot) * rows, rows)
            ch[at], cm[at] = parts2(source[g])
    moved, still = head_cols(flag_ref, q.shape[1])
    ga_ref[...] = mul3((ch[...], cm[...]), parts2(wo[...]), NT)
    gs_ref[...] = ga_ref[:, still]
    for g, (a, b) in enumerate(((rim_low, rim_first), (rim_last, rim_high))):
        rim = jnp.concatenate([a[...], b[...]], axis=0)
        half = left_ref.shape[0]
        at = pl.ds(g * half, half)
        gq, gkv = group_back(q[at], rim, pm[g], ga_ref[at, moved], scale)
        dq_ref[at] = gq
        if g == 0:
            left_ref[...] = gkv[:half]
            keep_ref[:half] = gkv[half:]
        else:
            keep_ref[half:] = gkv[:half]
            right_ref[...] = gkv[half:]


def still_back_kernel(scale, flag_ref, ga, kv, ps, q, dqm, wq, wk, wv, terms_ref, both):
    hd = dqm.shape[1]
    moved, still = head_cols(flag_ref, hd)
    gq, gkv = group_back(q[...], kv[...], ps[...], ga[...], scale)
    both[:, moved] = dqm[...]
    both[:, still] = gq
    terms_ref[...] = mul3(parts2(both[...]), parts2(wq[...]), NT)
    terms_ref[...] += mul3(parts2(gkv), parts2(cat(wk[:, still], wv[:, still])), NT)


def finish_kernel(flag_ref, wk, wv, terms_ref, keep_ref, left_ref, right_ref, mine_ref, theirs_ref):
    moved, _ = head_cols(flag_ref, wk.shape[1] // 2)
    rows = mine_ref.shape[1]
    grads = keep_ref[...] + jnp.concatenate([left_ref[...], right_ref[...]], axis=0)
    out = terms_ref[...] + mul3(parts2(grads), parts2(cat(wk[:, moved], wv[:, moved])), NT)
    for h in range(2):
        mine_ref[h] = out[2 * h * rows : (2 * h + 1) * rows]
        theirs_ref[h] = out[(2 * h + 1) * rows : (2 * h + 2) * rows]


class Fetched:
    def __init__(self, source, held, semaphore):
        self.copy, self.held, self.waiting = pltpu.make_async_copy(source, held, semaphore), held, True
        self.copy.start()

    @property
    def shape(self):
        return self.held.shape

    def __getitem__(self, at):
        if self.waiting:
            self.copy.wait()
            self.waiting = False
        return self.held[at]


def call(kernel, shapes, flag, operands, scratch=(), flops=0, fetched=0, away_out=False):
    vmem = pl.BlockSpec(memory_space=pltpu.VMEM)
    out = [s if isinstance(s, jax.ShapeDtypeStruct) else jax.ShapeDtypeStruct(s, F32) for s in shapes]
    away = operands[:fetched]

    def body(flag_ref, *refs):
        if away:
            sources, rest, held, semaphores = refs[:fetched], refs[fetched : -1 - fetched], refs[-1 - fetched : -1], refs[-1]
            refs = [Fetched(x, h, semaphores.at[i]) for i, (x, h) in enumerate(zip(sources, held))] + list(rest)
        kernel(flag_ref, *refs)

    return pl.pallas_call(
        body,
        out_shape=[pltpu.HBM(x.shape, x.dtype) for x in out] if away_out else out,
        in_specs=[pl.BlockSpec(memory_space=pltpu.SMEM)]
        + [pl.BlockSpec(memory_space=pltpu.HBM)] * fetched
        + [vmem] * (len(operands) - fetched),
        out_specs=[vmem] * len(shapes),
        scratch_shapes=list(scratch)
        + ([pltpu.VMEM(x.shape, x.dtype) for x in away] + [pltpu.SemaphoreType.DMA((fetched,))] if away else []),
        compiler_params=pltpu.CompilerParams(vmem_limit_bytes=LIMIT),
        cost_estimate=pl.CostEstimate(
            flops=int(flops),
            bytes_accessed=sum(x.dtype.itemsize * math.prod(x.shape) for x in [*out, *operands]),
            transcendentals=0,
        ),
    )(flag, *[pltpu.with_memory_space_constraint(x, pltpu.HBM) for x in away], *operands[fetched:])


LIMIT = 30 << 20


def rim_call(flag, own, other, gain, wk, wv):
    D, W = wk.shape
    T = 4 * own.shape[1]
    return call(
        rim_kernel, [(T // 2, W)] * 2 + [jax.ShapeDtypeStruct((T, D), BF16)] * 3,
        flag, [own, wk, wv, other, gain], flops=2 * T * D * W * 6,
    )


def still_call(scale, flag, parts, wq, wk, wv):
    D, W = wk.shape
    T, hd = parts[0].shape[0], W // 2
    return call(
        functools.partial(still_kernel, scale), [(T, hd)] * 2 + [(T, W), (T, T), (T, hd)],
        flag, [wk, wv, wq, *parts], scratch=[pltpu.VMEM((T, W), F32)], flops=2 * T * D * hd * 24 + 2 * T * T * hd * 9, away_out=True,
    )


def moved_call(scale, flag, q, first, last, low, high, out_still, wo):
    T, hd = out_still.shape
    D = wo.shape[1]
    return call(
        functools.partial(moved_kernel, scale), [(2, T // 2, T), (2, T // 4, D), (2, T // 4, D)],
        flag, [q, first, last, wo, out_still, low, high],
        scratch=[pltpu.VMEM((T, 2 * hd), F32)], flops=2 * T * D * hd * 6 + 2 * T * T * hd * 9, fetched=5,
    )


def moved_back_call(scale, flag, own, other, wo, q, first, last, low, high, pm):
    T, hd = q.shape
    D = wo.shape[1]
    return call(
        functools.partial(moved_back_kernel, scale),
        [(T, hd), (T, hd), (T // 2, 2 * hd), (T // 2, 2 * hd), (T, 2 * hd)],
        flag, [q, low, first, pm, last, high, own, other, wo],
        scratch=[pltpu.VMEM((T, D), BF16)] * 2 + [pltpu.VMEM((T, 2 * hd), F32)],
        flops=2 * T * D * hd * 6 + 2 * T * T * hd * 12, away_out=True,
    )


def still_back_call(scale, flag, ga, q, kv, ps, dqm, wq, wk, wv):
    T, hd = dqm.shape
    D = wq.shape[0]
    return call(
        functools.partial(still_back_kernel, scale), [(T, D)],
        flag, [ga, kv, ps, q, dqm, wq, wk, wv],
        scratch=[pltpu.VMEM((T, 2 * hd), F32)], flops=2 * T * D * hd * 12 + 2 * T * T * hd * 12, fetched=8,
    )[0]


def finish_call(flag, terms, keep, left, right, wk, wv):
    T, D = terms.shape
    return call(
        finish_kernel, [(2, T // 4, D)] * 2,
        flag, [wk, wv, terms, keep, left, right], flops=2 * T * D * wk.shape[1] * 3,
    )


CHIP = 2


def core_swap(x):
    length = lax.axis_size("head")
    return lax.ppermute(x, "head", [(i, i ^ 1) for i in range(length)])


def same_core():
    length = lax.axis_size("head")
    return [list(range(core, length, CHIP)) for core in range(CHIP)]


def gather_chips(rows):
    groups = same_core()
    chips = len(groups[0])
    sent = jnp.broadcast_to(rows[None], (chips,) + rows.shape)
    own = lax.all_to_all(sent, "head", 0, 0, tiled=True, axis_index_groups=groups)
    return own.reshape(2, -1, rows.shape[1])


def sum_chips(part):
    groups = same_core()
    chips = len(groups[0])
    split = part.reshape(chips, -1, part.shape[2])
    swapped = lax.all_to_all(split, "head", 0, 0, tiled=True, axis_index_groups=groups)
    return jnp.sum(swapped, axis=0)


def along(x, by):
    length = lax.axis_size("ctx")
    return lax.ppermute(x, "ctx", [(i, (i + by) % length) for i in range(length)])


def layer(tokens, norm_gain, w_query, w_key, w_value, w_out, shift_heads, cotangent):
    scale = 1.0 / math.sqrt(w_query.shape[1] // 2)
    flag = shift_heads[1:2]
    gain = norm_gain[None]
    own = gather_chips(tokens)
    own, cot_later = lax.optimization_barrier((own, cotangent))
    other = core_swap(own)
    cot_own = gather_chips(cot_later)
    first, last, *parts = rim_call(flag, own, other, gain, w_key, w_value)
    low, high = along(last, 1), along(first, -1)
    query_moved, query_still, kv_still, probs_still, out_still = still_call(scale, flag, parts, w_query, w_key, w_value)
    cot_own, out_still = lax.optimization_barrier((cot_own, out_still))
    cot_other = core_swap(cot_own)
    probs_moved, mine, theirs = moved_call(scale, flag, query_moved, first, last, low, high, out_still, w_out)
    out_part = mine + core_swap(theirs)
    grad_still, grad_query, left, right, keep = moved_back_call(
        scale, flag, cot_own, cot_other, w_out, query_moved, first, last, low, high, probs_moved
    )
    grad_query, out_part = lax.optimization_barrier((grad_query, out_part))
    out_sum = sum_chips(out_part)
    from_left, from_right = along(right, 1), along(left, -1)
    terms = still_back_call(
        scale, flag, grad_still, query_still, kv_still, probs_still, grad_query, w_query, w_key, w_value
    )
    mine, theirs = finish_call(flag, terms, keep, from_left, from_right, w_key, w_value)
    grad_part, out_sum = lax.optimization_barrier((mine + core_swap(theirs), out_sum))
    grad_sum = sum_chips(grad_part)
    mixed = tokens + out_sum
    inverse = lax.rsqrt(jnp.mean(tokens * tokens, axis=-1, keepdims=True) + 1e-06)
    weighted = grad_sum * norm_gain
    correction = jnp.mean(weighted * tokens, axis=-1, keepdims=True)
    input_grad = (
        cotangent + weighted * inverse - tokens * (inverse * inverse * inverse) * correction
    )
    return (mixed, input_grad)


def solution(mesh):
    placed = (
        P(("ctx", "head"), None),
        P(),
        P(None, "head"),
        P(None, "head"),
        P(None, "head"),
        P("head", None),
        P("head"),
        P(("ctx", "head"), None),
    )
    return jax.shard_map(
        layer,
        mesh=mesh,
        in_specs=placed,
        out_specs=(P(("ctx", "head"), None), P(("ctx", "head"), None)),
        check_vma=False,
    )
```

time: 183 us -> 184 us (level)
  the two profiles are of different devices: /device:TPU:6 before, /device:TPU:40 now
where the time goes in v2:
time: 184 us; the launch traced here: 183 us
  blocking collectives  85.3 us (46%)
  starting transfers between devices  42.3 us (23%)
  Pallas kernels  29.3 us (16%)
  waiting for transfers between devices  19 us (10%)
  local copies, waits for them, and re-layouts  3.95 us (2%)
  other arithmetic  2.26 us (1%)
    all_to_all x1, blocking collectives, sum_chips(): lax.all_to_all(split, 'head', 0, 0, tiled=True, axis_index_groups=groups)  45.9 us
    all_to_all x1, blocking collectives, gather_chips(): lax.all_to_all(sent, 'head', 0, 0, tiled=True, axis_index_groups=groups)  39.4 us
    pallas_call x6, Pallas kernels, call(): pl.pallas_call(body, out_shape=[pltpu.HBM(x.shape, x.dtype) for x in out]...  29.3 us
    ppermute x4, starting transfers between devices, along(): lax.ppermute(x, 'ctx', [(i, (i + by) % length) for i in range(length)])  20.7 us
    ppermute x4, waiting for transfers between devices, along(): lax.ppermute(x, 'ctx', [(i, (i + by) % length) for i in range(length)])  12.5 us
    all_to_all x1, starting transfers between devices, sum_chips(): lax.all_to_all(split, 'head', 0, 0, tiled=True, axis_index_groups=groups)  9.31 us
    ppermute x4, starting transfers between devices, core_swap(): return lax.ppermute(x, 'head', [(i, i ^ 1) for i in range(length)])  8.29 us
    ppermute x4, waiting for transfers between devices, core_swap(): return lax.ppermute(x, 'head', [(i, i ^ 1) for i in range(length)])  5.8 us
  transfers between devices with their start and end apart: 10, of which 7 were waited for; matrix products, arithmetic and copies ran while one was open for 1% of the time, Pallas kernels for 10%

profile of v2, /device:TPU:40, one launch (start us, length us, event | category | flops | bytes accessed | tf_op | source)
XLA Modules:
  0.0 183.0 jit_solution(15241471569683857504)
XLA Ops:
  0.6 0.0 copy-start.16
  0.6 1.0 broadcast_in_dim.6
  1.6 39.4 %all_to_all.20 = f32[16,16,1024]{2,1,0:T(8,128)S(1)} all-to-all(f32[16,16,1024]{2,1,0:T(8,128)S(1)} %broadcast_in_dim.6), channel_id=1, replica_groups={{0,2,4,6,8,10,12,14,16,18,20,22,24,26,28,30},{1,3,5,7,9,11,13,15,17,19,..., dimensions={0} | all-to-all | bytes 2097152 | tf_op jit(solution)/shard_map/all_to_all | solution.py:306
  41.0 0.0 copy-done.16
  41.0 1.1 broadcast_in_dim.8
  42.1 4.0 %all-to-all-start.1 = ((f32[16,16,1024]{2,1,0:T(8,128)}), f32[16,16,1024]{2,1,0:T(8,128)S(1)}, u32[]{:S(2)}, u32[]{:S(2)}) async-start(f32[16,16,1024]{2,1,0:T(8,128)} %broadcast_in_dim.8), calls=%async_computation.1 | async-start | bytes 2097152 | tf_op jit(solution)/shard_map/all_to_all | solution.py:306
  46.0 1.9 %collective-permute-start = (f32[2,128,1024]{2,1,0:T(8,128)S(1)}, f32[2,128,1024]{2,1,0:T(8,128)S(1)}, u32[]{:S(2)}, u32[]{:S(2)}) collective-permute-start(f32[2,128,1024]{2,1,0:T(8,128)S(1)} %bitcast.7), channel_id=1, source_target_pairs={{0,1},{1,0},{2,3},{3,2},{4,5},{5,4},{6,7},{7,6},{8,9},{9,8},{10,11... | collective-permute-start | bytes 3145736 | tf_op jit(solution)/shard_map/ppermute | solution.py:294
  48.0 0.0 copy-done.19
  48.0 0.6 slice.3.flag_ref
  48.6 2.0 %collective-permute-done.refs_3_ = f32[2,128,1024]{2,1,0:T(8,128)S(1)} collective-permute-done((f32[2,128,1024]{2,1,0:T(8,128)S(1)}, f32[2,128,1024]{2,1,0:T(8,128)S(1)}, u32[]{:S(2)}, u32[]{:S(2)}) %collective-permute-start) | collective-permute-done | bytes 1048608 | tf_op jit(solution)/shard_map/ppermute | solution.py:294
  50.6 0.0 copy-done
  50.6 1.2 copy-done.2
  51.8 4.3 %shard_map.95 = (f32[256,256]{1,0:T(8,128)S(1)}, f32[256,256]{1,0:T(8,128)}, bf16[512,1024]{1,0:T(8,128)(2,1)S(1)}, bf16[512,1024]{1,0:T(8,128)(2,1)S(1)}, bf16[512,1024]{1,0:T(8,128)(2,1)S(1)}) custom-call(s32[1]{0:T(128)} %slice.3.flag_ref, f32[2,128,1024]{2,1,0:T(8,128)S(1)} %bitcast.8, f32[1024,256]{1,0:T(8,128)S(1)} %copy-done, ...), custom_call_target="tpu_custom_call" | custom-call | flops 1610612736 | bytes 7868416 | tf_op jit(solution)/shard_map/pallas_call | solution.py:210
  56.1 3.4 %collective-permute-start.1 = (f32[256,256]{1,0:T(8,128)}, f32[256,256]{1,0:T(8,128)S(1)}, u32[]{:S(2)}, u32[]{:S(2)}) collective-permute-start(f32[256,256]{1,0:T(8,128)} %get-tuple-element.35.refs_2_.refs_4_), channel_id=1, source_target_pairs={{0,32},{32,64},{64,96},{96,128},{128,160},{160,192},{192,224},{224... | collective-permute-start | bytes 786440 | tf_op jit(solution)/shard_map/ppermute | solution.py:320
  59.5 6.7 %collective-permute-start.2 = (f32[256,256]{1,0:T(8,128)S(1)}, f32[256,256]{1,0:T(8,128)S(1)}, u32[]{:S(2)}, u32[]{:S(2)}) collective-permute-start(f32[256,256]{1,0:T(8,128)S(1)} %get-tuple-element.36.refs_1_.refs_2_), channel_id=1, source_target_pairs={{0,480},{32,0},{64,32},{96,64},{128,96},{160,128},{192,160},{224,1... | collective-permute-start | bytes 786440 | tf_op jit(solution)/shard_map/ppermute | solution.py:320
  66.2 6.3 %shard_map.96 = (f32[512,128]{1,0:T(8,128)}, f32[512,128]{1,0:T(8,128)}, f32[512,256]{1,0:T(8,128)}, f32[512,512]{1,0:T(8,128)}, f32[512,128]{1,0:T(8,128)}) custom-call(s32[1]{0:T(128)} %slice.3.flag_ref, f32[1024,256]{1,0:T(8,128)S(1)} %copy-done, f32[1024,256]{1,0:T(8,128)S(1)} %copy-done.2, f32[1024,256]{1,0:T(8,128)S(1)} %copy-done.7, ...), custom_call_target="tpu_custom_call" | custom-call | flops 3825205248 | bytes 8650752 | tf_op jit(solution)/shard_map/pallas_call | solution.py:210
  72.5 0.0 copy-done.8
  72.5 0.7 all-to-all-done.1
  73.2 0.0 collective-permute-done.1.refs_5_.refs_1_
  73.2 2.3 %collective-permute-done.2.refs_6_.refs_5_ = f32[256,256]{1,0:T(8,128)S(1)} collective-permute-done((f32[256,256]{1,0:T(8,128)S(1)}, f32[256,256]{1,0:T(8,128)S(1)}, u32[]{:S(2)}, u32[]{:S(2)}) %collective-permute-start.2) | collective-permute-done | bytes 262176 | tf_op jit(solution)/shard_map/ppermute | solution.py:320
  75.5 4.5 %shard_map.97 = (f32[2,256,512]{2,1,0:T(8,128)S(1)}, f32[2,128,1024]{2,1,0:T(8,128)S(1)}, f32[2,128,1024]{2,1,0:T(8,128)S(1)}) custom-call(s32[1]{0:T(128)} %slice.3.flag_ref, f32[512,128]{1,0:T(8,128)} %get-tuple-element.34.refs_0_, f32[256,256]{1,0:T(8,128)} %copy-done.8, f32[256,256]{1,0:T(8,128)} %get-tuple-element.35.refs_2_.refs_4_, ...), custom_call_target="tpu_custom_call" | custom-call | flops 1409286144 | bytes 5767168 | tf_op jit(solution)/shard_map/pallas_call | solution.py:210
  80.1 0.0 copy-start.6
  80.1 2.1 %collective-permute-start.4 = (f32[2,128,1024]{2,1,0:T(8,128)S(1)}, f32[2,128,1024]{2,1,0:T(8,128)S(1)}, u32[]{:S(2)}, u32[]{:S(2)}) collective-permute-start(f32[2,128,1024]{2,1,0:T(8,128)S(1)} %get-tuple-element.48), channel_id=1, source_target_pairs={{0,1},{1,0},{2,3},{3,2},{4,5},{5,4},{6,7},{7,6},{8,9},{9,8},{10,11... | collective-permute-start | bytes 3145736 | tf_op jit(solution)/shard_map/ppermute | solution.py:294
  82.2 2.4 %collective-permute-start.3 = (f32[2,128,1024]{2,1,0:T(8,128)S(1)}, f32[2,128,1024]{2,1,0:T(8,128)S(1)}, u32[]{:S(2)}, u32[]{:S(2)}) collective-permute-start(f32[2,128,1024]{2,1,0:T(8,128)S(1)} %bitcast.5), channel_id=1, source_target_pairs={{0,1},{1,0},{2,3},{3,2},{4,5},{5,4},{6,7},{7,6},{8,9},{9,8},{10,11... | collective-permute-start | bytes 3145736 | tf_op jit(solution)/shard_map/ppermute | solution.py:294
  84.6 0.2 collective-permute-done.4
  84.8 1.1 add.23
  85.9 0.9 collective-permute-done.3.refs_7_
  86.9 0.0 copy-done.11
  86.9 6.5 %shard_map.98 = (f32[512,128]{1,0:T(8,128)}, f32[512,128]{1,0:T(8,128)}, f32[256,256]{1,0:T(8,128)}, f32[256,256]{1,0:T(8,128)}, f32[512,256]{1,0:T(8,128)}) custom-call(s32[1]{0:T(128)} %slice.3.flag_ref, f32[512,128]{1,0:T(8,128)S(1)} %copy-done.14, f32[256,256]{1,0:T(8,128)S(1)} %copy-done.11, f32[256,256]{1,0:T(8,128)S(1)} %copy-done.9, ...), custom_call_target="tpu_custom_call" | custom-call | flops 1610612736 | bytes 7077888 | tf_op jit(solution)/shard_map/pallas_call | solution.py:210
  93.4 9.3 %all-to-all-start.2 = ((f32[16,16,1024]{2,1,0:T(8,128)}), f32[16,16,1024]{2,1,0:T(8,128)S(1)}, u32[]{:S(2)}, u32[]{:S(2)}) async-start(f32[16,16,1024]{2,1,0:T(8,128)} %bitcast.3), calls=%async_computation.2 | async-start | bytes 2097152 | tf_op jit(solution)/shard_map/all_to_all | solution.py:314
  102.7 2.1 %collective-permute-start.5 = (f32[256,256]{1,0:T(8,128)S(1)}, f32[256,256]{1,0:T(8,128)S(1)}, u32[]{:S(2)}, u32[]{:S(2)}) collective-permute-start(f32[256,256]{1,0:T(8,128)S(1)} %copy-done.18), channel_id=1, source_target_pairs={{0,32},{32,64},{64,96},{96,128},{128,160},{160,192},{192,224},{224... | collective-permute-start | bytes 786440 | tf_op jit(solution)/shard_map/ppermute | solution.py:320
  104.9 8.6 %collective-permute-start.6 = (f32[256,256]{1,0:T(8,128)S(1)}, f32[256,256]{1,0:T(8,128)S(1)}, u32[]{:S(2)}, u32[]{:S(2)}) collective-permute-start(f32[256,256]{1,0:T(8,128)S(1)} %copy-done.17), channel_id=1, source_target_pairs={{0,480},{32,0},{64,32},{96,64},{128,96},{160,128},{192,160},{224,1... | collective-permute-start | bytes 786440 | tf_op jit(solution)/shard_map/ppermute | solution.py:320
  113.4 0.0 copy-start.1
  113.5 0.0 copy-start.3
  113.5 6.0 %shard_map.99.refs_2_ = f32[512,1024]{1,0:T(8,128)S(1)} custom-call(s32[1]{0:T(128)} %slice.3.flag_ref, f32[512,128]{1,0:T(8,128)} %get-tuple-element.42.refs_0_, f32[512,256]{1,0:T(8,128)} %get-tuple-element.43.refs_1_, f32[512,512]{1,0:T(8,128)} %get-tuple-element.44.refs_2_, f32[512,128]{1,0:T(8,128)} %get-tuple-element.45.refs_3_, ...), custom_call_target="tpu_custom_call" | custom-call | flops 2415919104 | bytes 7602176 | tf_op jit(solution)/shard_map/pallas_call | solution.py:210
  119.5 0.0 collective-permute-done.5.refs_4_
  119.5 10.1 %collective-permute-done.6.refs_5_ = f32[256,256]{1,0:T(8,128)S(1)} collective-permute-done((f32[256,256]{1,0:T(8,128)S(1)}, f32[256,256]{1,0:T(8,128)S(1)}, u32[]{:S(2)}, u32[]{:S(2)}) %collective-permute-start.6) | collective-permute-done | bytes 262176 | tf_op jit(solution)/shard_map/ppermute | solution.py:320
  129.6 1.7 shard_map.100
  131.3 1.9 %collective-permute-start.7 = (f32[2,128,1024]{2,1,0:T(8,128)S(1)}, f32[2,128,1024]{2,1,0:T(8,128)S(1)}, u32[]{:S(2)}, u32[]{:S(2)}) collective-permute-start(f32[2,128,1024]{2,1,0:T(8,128)S(1)} %get-tuple-element.54), channel_id=1, source_target_pairs={{0,1},{1,0},{2,3},{3,2},{4,5},{5,4},{6,7},{7,6},{8,9},{9,8},{10,11... | collective-permute-start | bytes 3145736 | tf_op jit(solution)/shard_map/ppermute | solution.py:294
  133.3 2.6 %collective-permute-done.7 = f32[2,128,1024]{2,1,0:T(8,128)S(1)} collective-permute-done((f32[2,128,1024]{2,1,0:T(8,128)S(1)}, f32[2,128,1024]{2,1,0:T(8,128)S(1)}, u32[]{:S(2)}, u32[]{:S(2)}) %collective-permute-start.7) | collective-permute-done | bytes 1048608 | tf_op jit(solution)/shard_map/ppermute | solution.py:294
  135.9 0.2 add.24
  136.1 0.0 copy-start.15
  136.1 0.0 all-to-all-done.2
  136.1 0.1 reduce_sum.36
  136.2 45.9 %all_to_all.21 = f32[16,16,1024]{2,1,0:T(8,128)S(1)} all-to-all(f32[16,16,1024]{2,1,0:T(8,128)S(1)} %bitcast.10), channel_id=1, replica_groups={{0,2,4,6,8,10,12,14,16,18,20,22,24,26,28,30},{1,3,5,7,9,11,13,15,17,19,..., dimensions={0} | all-to-all | bytes 2097152 | tf_op jit(solution)/shard_map/all_to_all | solution.py:314
  182.1 0.1 reduce_sum.37
  182.1 0.1 multiply_reduce_fusion.1
  182.3 0.7 multiply_subtract_fusion
  (30 shorter events, 0.1 us)
Async XLA Ops:
  0.6 40.4 %copy-start.16 = (f32[16,1024]{1,0:T(8,128)S(1)}, f32[16,1024]{1,0:T(8,128)}, u32[]{:S(2)}) copy-start(f32[16,1024]{1,0:T(8,128)} %param.15) | copy-start | bytes 196612
  41.0 7.0 %copy-start.19 = (s32[2]{0:T(128)S(1)}, s32[2]{0:T(128)}, u32[]{:S(2)}) copy-start(s32[2]{0:T(128)} %param.14) | copy-start | bytes 28
  41.0 9.6 %copy-start = (f32[1024,256]{1,0:T(8,128)S(1)}, f32[1024,256]{1,0:T(8,128)}, u32[]{:S(2)}) copy-start(f32[1024,256]{1,0:T(8,128)} %refs_0_.3) | copy-start | bytes 3145732
  41.0 9.6 %copy-start.5 = (f32[1024]{0:T(1024)S(1)}, f32[1024]{0:T(1024)}, u32[]{:S(2)}) copy-start(f32[1024]{0:T(1024)} %param.9) | copy-start | bytes 12292
  42.1 31.1 %all-to-all-start.1 = ((f32[16,16,1024]{2,1,0:T(8,128)}), f32[16,16,1024]{2,1,0:T(8,128)S(1)}, u32[]{:S(2)}, u32[]{:S(2)}) async-start(f32[16,16,1024]{2,1,0:T(8,128)} %broadcast_in_dim.8), calls=%async_computation.1 | async-start | bytes 2097152 | tf_op jit(solution)/shard_map/all_to_all | solution.py:306
  46.0 4.5 %collective-permute-start = (f32[2,128,1024]{2,1,0:T(8,128)S(1)}, f32[2,128,1024]{2,1,0:T(8,128)S(1)}, u32[]{:S(2)}, u32[]{:S(2)}) collective-permute-start(f32[2,128,1024]{2,1,0:T(8,128)S(1)} %bitcast.7), channel_id=1, source_target_pairs={{0,1},{1,0},{2,3},{3,2},{4,5},{5,4},{6,7},{7,6},{8,9},{9,8},{10,11... | collective-permute-start | bytes 3145736 | tf_op jit(solution)/shard_map/ppermute | solution.py:294
  50.6 1.2 copy-start.2
  51.8 14.4 %copy-start.7 = (f32[1024,256]{1,0:T(8,128)S(1)}, f32[1024,256]{1,0:T(8,128)}, u32[]{:S(2)}) copy-start(f32[1024,256]{1,0:T(8,128)} %refs_5_.1) | copy-start | bytes 3145732
  56.1 16.4 %copy-start.8 = (f32[256,256]{1,0:T(8,128)}, f32[256,256]{1,0:T(8,128)S(1)}, u32[]{:S(2)}) copy-start(f32[256,256]{1,0:T(8,128)S(1)} %get-tuple-element.36.refs_1_.refs_2_) | copy-start | bytes 786436
  56.1 17.1 %collective-permute-start.1 = (f32[256,256]{1,0:T(8,128)}, f32[256,256]{1,0:T(8,128)S(1)}, u32[]{:S(2)}, u32[]{:S(2)}) collective-permute-start(f32[256,256]{1,0:T(8,128)} %get-tuple-element.35.refs_2_.refs_4_), channel_id=1, source_target_pairs={{0,32},{32,64},{64,96},{96,128},{128,160},{160,192},{192,224},{224... | collective-permute-start | bytes 786440 | tf_op jit(solution)/shard_map/ppermute | solution.py:320
  59.5 16.0 %collective-permute-start.2 = (f32[256,256]{1,0:T(8,128)S(1)}, f32[256,256]{1,0:T(8,128)S(1)}, u32[]{:S(2)}, u32[]{:S(2)}) collective-permute-start(f32[256,256]{1,0:T(8,128)S(1)} %get-tuple-element.36.refs_1_.refs_2_), channel_id=1, source_target_pairs={{0,480},{32,0},{64,32},{96,64},{128,96},{160,128},{192,160},{224,1... | collective-permute-start | bytes 786440 | tf_op jit(solution)/shard_map/ppermute | solution.py:320
  73.2 6.9 %copy-start.10 = (f32[256,256]{1,0:T(8,128)}, f32[256,256]{1,0:T(8,128)S(1)}, u32[]{:S(2)}) copy-start(f32[256,256]{1,0:T(8,128)S(1)} %collective-permute-done.1.refs_5_.refs_1_) | copy-start | bytes 786436
  75.5 4.5 %copy-start.12 = (f32[256,256]{1,0:T(8,128)}, f32[256,256]{1,0:T(8,128)S(1)}, u32[]{:S(2)}) copy-start(f32[256,256]{1,0:T(8,128)S(1)} %collective-permute-done.2.refs_6_.refs_5_) | copy-start | bytes 786436
  80.1 6.8 %copy-start.6 = (f32[256,1024]{1,0:T(8,128)S(1)}, f32[256,1024]{1,0:T(8,128)}, u32[]{:S(2)}) copy-start(f32[256,1024]{1,0:T(8,128)} %refs_8_.1) | copy-start | bytes 3145732
  80.1 6.8 %copy-start.9 = (f32[256,256]{1,0:T(8,128)S(1)}, f32[256,256]{1,0:T(8,128)}, u32[]{:S(2)}) copy-start(f32[256,256]{1,0:T(8,128)} %copy-done.8) | copy-start | bytes 786436
  80.1 6.8 %copy-start.14 = (f32[512,128]{1,0:T(8,128)S(1)}, f32[512,128]{1,0:T(8,128)}, u32[]{:S(2)}) copy-start(f32[512,128]{1,0:T(8,128)} %get-tuple-element.34.refs_0_) | copy-start | bytes 786436
  80.1 6.8 %copy-start.11 = (f32[256,256]{1,0:T(8,128)S(1)}, f32[256,256]{1,0:T(8,128)}, u32[]{:S(2)}) copy-start(f32[256,256]{1,0:T(8,128)} %copy-done.10) | copy-start | bytes 786436
  80.1 6.8 %copy-start.13 = (f32[256,256]{1,0:T(8,128)S(1)}, f32[256,256]{1,0:T(8,128)}, u32[]{:S(2)}) copy-start(f32[256,256]{1,0:T(8,128)} %copy-done.12) | copy-start | bytes 786436
  80.1 4.7 %collective-permute-start.4 = (f32[2,128,1024]{2,1,0:T(8,128)S(1)}, f32[2,128,1024]{2,1,0:T(8,128)S(1)}, u32[]{:S(2)}, u32[]{:S(2)}) collective-permute-start(f32[2,128,1024]{2,1,0:T(8,128)S(1)} %get-tuple-element.48), channel_id=1, source_target_pairs={{0,1},{1,0},{2,3},{3,2},{4,5},{5,4},{6,7},{7,6},{8,9},{9,8},{10,11... | collective-permute-start | bytes 3145736 | tf_op jit(solution)/shard_map/ppermute | solution.py:294
  82.2 4.7 %collective-permute-start.3 = (f32[2,128,1024]{2,1,0:T(8,128)S(1)}, f32[2,128,1024]{2,1,0:T(8,128)S(1)}, u32[]{:S(2)}, u32[]{:S(2)}) collective-permute-start(f32[2,128,1024]{2,1,0:T(8,128)S(1)} %bitcast.5), channel_id=1, source_target_pairs={{0,1},{1,0},{2,3},{3,2},{4,5},{5,4},{6,7},{7,6},{8,9},{9,8},{10,11... | collective-permute-start | bytes 3145736 | tf_op jit(solution)/shard_map/ppermute | solution.py:294
  93.4 9.3 %copy-start.18 = (f32[256,256]{1,0:T(8,128)S(1)}, f32[256,256]{1,0:T(8,128)}, u32[]{:S(2)}) copy-start(f32[256,256]{1,0:T(8,128)} %get-tuple-element.51) | copy-start | bytes 786436
  93.4 11.4 %copy-start.17 = (f32[256,256]{1,0:T(8,128)S(1)}, f32[256,256]{1,0:T(8,128)}, u32[]{:S(2)}) copy-start(f32[256,256]{1,0:T(8,128)} %get-tuple-element.52) | copy-start | bytes 786436
  93.4 42.7 %all-to-all-start.2 = ((f32[16,16,1024]{2,1,0:T(8,128)}), f32[16,16,1024]{2,1,0:T(8,128)S(1)}, u32[]{:S(2)}, u32[]{:S(2)}) async-start(f32[16,16,1024]{2,1,0:T(8,128)} %bitcast.3), calls=%async_computation.2 | async-start | bytes 2097152 | tf_op jit(solution)/shard_map/all_to_all | solution.py:314
  102.7 16.8 %collective-permute-start.5 = (f32[256,256]{1,0:T(8,128)S(1)}, f32[256,256]{1,0:T(8,128)S(1)}, u32[]{:S(2)}, u32[]{:S(2)}) collective-permute-start(f32[256,256]{1,0:T(8,128)S(1)} %copy-done.18), channel_id=1, source_target_pairs={{0,32},{32,64},{64,96},{96,128},{128,160},{160,192},{192,224},{224... | collective-permute-start | bytes 786440 | tf_op jit(solution)/shard_map/ppermute | solution.py:320
  104.9 24.8 %collective-permute-start.6 = (f32[256,256]{1,0:T(8,128)S(1)}, f32[256,256]{1,0:T(8,128)S(1)}, u32[]{:S(2)}, u32[]{:S(2)}) collective-permute-start(f32[256,256]{1,0:T(8,128)S(1)} %copy-done.17), channel_id=1, source_target_pairs={{0,480},{32,0},{64,32},{96,64},{128,96},{160,128},{192,160},{224,1... | collective-permute-start | bytes 786440 | tf_op jit(solution)/shard_map/ppermute | solution.py:320
  113.4 16.2 %copy-start.1 = (f32[1024,256]{1,0:T(8,128)S(1)}, f32[1024,256]{1,0:T(8,128)}, u32[]{:S(2)}) copy-start(f32[1024,256]{1,0:T(8,128)} %refs_0_.3) | copy-start | bytes 3145732
  113.5 16.2 %copy-start.3 = (f32[1024,256]{1,0:T(8,128)S(1)}, f32[1024,256]{1,0:T(8,128)}, u32[]{:S(2)}) copy-start(f32[1024,256]{1,0:T(8,128)} %refs_1_.5) | copy-start | bytes 3145732
  113.5 16.2 %copy-start.4 = (f32[512,256]{1,0:T(8,128)S(1)}, f32[512,256]{1,0:T(8,128)}, u32[]{:S(2)}) copy-start(f32[512,256]{1,0:T(8,128)} %get-tuple-element.50.refs_3_) | copy-start | bytes 1572868
  131.3 4.6 %collective-permute-start.7 = (f32[2,128,1024]{2,1,0:T(8,128)S(1)}, f32[2,128,1024]{2,1,0:T(8,128)S(1)}, u32[]{:S(2)}, u32[]{:S(2)}) collective-permute-start(f32[2,128,1024]{2,1,0:T(8,128)S(1)} %get-tuple-element.54), channel_id=1, source_target_pairs={{0,1},{1,0},{2,3},{3,2},{4,5},{5,4},{6,7},{7,6},{8,9},{9,8},{10,11... | collective-permute-start | bytes 3145736 | tf_op jit(solution)/shard_map/ppermute | solution.py:294
  136.1 46.1 %copy-start.15 = (f32[16,1024]{1,0:T(8,128)S(1)}, f32[16,1024]{1,0:T(8,128)}, u32[]{:S(2)}) copy-start(f32[16,1024]{1,0:T(8,128)} %param.8) | copy-start | bytes 196612

commit v3 on v2

--- a/solution.py
+++ b/solution.py
@@ -66,8 +66,10 @@
 
 
 def normed_parts(own, other, gain_ref, refs):
-    for slot, source in enumerate((own, other)):
+    for slot, source in ((1, other), (0, own)):
         rows = source.shape[1]
+        if isinstance(source, Fetched):
+            source = source.ready()
 
         @pl.loop(0, 2)
         def _(half):
@@ -189,11 +191,14 @@
     def shape(self):
         return self.held.shape
 
-    def __getitem__(self, at):
+    def ready(self):
         if self.waiting:
             self.copy.wait()
             self.waiting = False
-        return self.held[at]
+        return self.held
+
+    def __getitem__(self, at):
+        return self.ready()[at]
 
 
 def call(kernel, shapes, flag, operands, scratch=(), flops=0, fetched=0, away_out=False):
@@ -233,7 +238,7 @@
     T = 4 * own.shape[1]
     return call(
         rim_kernel, [(T // 2, W)] * 2 + [jax.ShapeDtypeStruct((T, D), BF16)] * 3,
-        flag, [own, wk, wv, other, gain], flops=2 * T * D * W * 6,
+        flag, [own, wk, wv, other, gain], flops=2 * T * D * W * 6, fetched=3,
     )
 
 

time: 184 us -> 185 us (level)
  Pallas kernels: 29.3 us -> 31.7 us
    pallas_call x6, Pallas kernels: 29.3 us -> 31.7 us  [call(): pl.pallas_call(body, out_shape=[pltpu.HBM(x.shape, x.dtype) for x in out]...]
  transfers between devices with their start and end apart: 10 -> 10, of which waited for: 7 -> 6; matrix products, arithmetic and copies ran while one was open for 1% -> 1% of each run, Pallas kernels for 10% -> 11%
where the time goes in v3:
time: 185 us; the launch traced here: 184 us
  blocking collectives  85.2 us (46%)
  starting transfers between devices  42.4 us (23%)
  Pallas kernels  31.7 us (17%)
  waiting for transfers between devices  18.8 us (10%)
  local copies, waits for them, and re-layouts  2.88 us (2%)
  other arithmetic  2.31 us (1%)
    all_to_all x1, blocking collectives, sum_chips(): lax.all_to_all(split, 'head', 0, 0, tiled=True, axis_index_groups=groups)  45.8 us
    all_to_all x1, blocking collectives, gather_chips(): lax.all_to_all(sent, 'head', 0, 0, tiled=True, axis_index_groups=groups)  39.4 us
    pallas_call x6, Pallas kernels, call(): pl.pallas_call(body, out_shape=[pltpu.HBM(x.shape, x.dtype) for x in out]...  31.7 us
    ppermute x4, starting transfers between devices, along(): lax.ppermute(x, 'ctx', [(i, (i + by) % length) for i in range(length)])  20.7 us
    ppermute x4, waiting for transfers between devices, along(): lax.ppermute(x, 'ctx', [(i, (i + by) % length) for i in range(length)])  12.5 us
    all_to_all x1, starting transfers between devices, sum_chips(): lax.all_to_all(split, 'head', 0, 0, tiled=True, axis_index_groups=groups)  9.31 us
    ppermute x4, starting transfers between devices, core_swap(): return lax.ppermute(x, 'head', [(i, i ^ 1) for i in range(length)])  8.47 us
    ppermute x4, waiting for transfers between devices, core_swap(): return lax.ppermute(x, 'head', [(i, i ^ 1) for i in range(length)])  5.58 us
  transfers between devices with their start and end apart: 10, of which 6 were waited for; matrix products, arithmetic and copies ran while one was open for 1% of the time, Pallas kernels for 11%

profile of v3, /device:TPU:40, one launch (start us, length us, event | category | flops | bytes accessed | tf_op | source)
XLA Modules:
  0.0 184.2 jit_solution(3532106362301609302)
XLA Ops:
  0.6 0.0 copy-start.13
  0.6 1.0 broadcast_in_dim.6
  1.6 39.4 %all_to_all.20 = f32[16,16,1024]{2,1,0:T(8,128)S(1)} all-to-all(f32[16,16,1024]{2,1,0:T(8,128)S(1)} %broadcast_in_dim.6), channel_id=1, replica_groups={{0,2,4,6,8,10,12,14,16,18,20,22,24,26,28,30},{1,3,5,7,9,11,13,15,17,19,..., dimensions={0} | all-to-all | bytes 2097152 | tf_op jit(solution)/shard_map/all_to_all | solution.py:311
  41.0 0.0 copy-done.13
  41.0 1.2 broadcast_in_dim.8
  42.2 4.0 %all-to-all-start.1 = ((f32[16,16,1024]{2,1,0:T(8,128)}), f32[16,16,1024]{2,1,0:T(8,128)S(1)}, u32[]{:S(2)}, u32[]{:S(2)}) async-start(f32[16,16,1024]{2,1,0:T(8,128)} %broadcast_in_dim.8), calls=%async_computation.1 | async-start | bytes 2097152 | tf_op jit(solution)/shard_map/all_to_all | solution.py:311
  46.2 1.9 %collective-permute-start = (f32[2,128,1024]{2,1,0:T(8,128)S(1)}, f32[2,128,1024]{2,1,0:T(8,128)S(1)}, u32[]{:S(2)}, u32[]{:S(2)}) collective-permute-start(f32[2,128,1024]{2,1,0:T(8,128)S(1)} %bitcast.9), channel_id=1, source_target_pairs={{0,1},{1,0},{2,3},{3,2},{4,5},{5,4},{6,7},{7,6},{8,9},{9,8},{10,11... | collective-permute-start | bytes 3145736 | tf_op jit(solution)/shard_map/ppermute | solution.py:299
  48.1 0.0 copy-done.16
  48.1 0.6 slice.3.flag_ref
  48.7 2.0 %collective-permute-done.refs_3_ = f32[2,128,1024]{2,1,0:T(8,128)S(1)} collective-permute-done((f32[2,128,1024]{2,1,0:T(8,128)S(1)}, f32[2,128,1024]{2,1,0:T(8,128)S(1)}, u32[]{:S(2)}, u32[]{:S(2)}) %collective-permute-start) | collective-permute-done | bytes 1048608 | tf_op jit(solution)/shard_map/ppermute | solution.py:299
  50.8 0.0 copy-done.11
  50.8 0.0 copy-done.5
  50.8 0.0 copy-start.7
  50.8 5.5 %shard_map.95 = (f32[256,256]{1,0:T(8,128)S(1)}, f32[256,256]{1,0:T(8,128)}, bf16[512,1024]{1,0:T(8,128)(2,1)S(1)}, bf16[512,1024]{1,0:T(8,128)(2,1)S(1)}, bf16[512,1024]{1,0:T(8,128)(2,1)S(1)}) custom-call(s32[1]{0:T(128)} %slice.3.flag_ref, f32[2,128,1024]{2,1,0:T(8,128)} %bitcast.10, f32[1024,256]{1,0:T(8,128)} %refs_0_.3, f32[1024,256]{1,0:T(8,128)} %refs_1_.5, ...), custom_call_target="tpu_custom_call" | custom-call | flops 1610612736 | bytes 7868416 | tf_op jit(solution)/shard_map/pallas_call | solution.py:215
  56.2 0.0 copy-start.8
  56.3 3.4 %collective-permute-start.1 = (f32[256,256]{1,0:T(8,128)}, f32[256,256]{1,0:T(8,128)}, u32[]{:S(2)}, u32[]{:S(2)}) collective-permute-start(f32[256,256]{1,0:T(8,128)} %get-tuple-element.35.refs_2_.refs_4_), channel_id=1, source_target_pairs={{0,32},{32,64},{64,96},{96,128},{128,160},{160,192},{192,224},{224... | collective-permute-start | bytes 786440 | tf_op jit(solution)/shard_map/ppermute | solution.py:325
  59.7 6.7 %collective-permute-start.2 = (f32[256,256]{1,0:T(8,128)S(1)}, f32[256,256]{1,0:T(8,128)}, u32[]{:S(2)}, u32[]{:S(2)}) collective-permute-start(f32[256,256]{1,0:T(8,128)S(1)} %get-tuple-element.36.refs_1_.refs_2_), channel_id=1, source_target_pairs={{0,480},{32,0},{64,32},{96,64},{128,96},{160,128},{192,160},{224,1... | collective-permute-start | bytes 786440 | tf_op jit(solution)/shard_map/ppermute | solution.py:325
  66.4 6.3 %shard_map.96 = (f32[512,128]{1,0:T(8,128)}, f32[512,128]{1,0:T(8,128)}, f32[512,256]{1,0:T(8,128)}, f32[512,512]{1,0:T(8,128)}, f32[512,128]{1,0:T(8,128)}) custom-call(s32[1]{0:T(128)} %slice.3.flag_ref, f32[1024,256]{1,0:T(8,128)S(1)} %copy-done, f32[1024,256]{1,0:T(8,128)S(1)} %copy-done.2, f32[1024,256]{1,0:T(8,128)S(1)} %copy-done.7, ...), custom_call_target="tpu_custom_call" | custom-call | flops 3825205248 | bytes 8650752 | tf_op jit(solution)/shard_map/pallas_call | solution.py:215
  72.7 0.7 all-to-all-done.1
  73.4 0.0 collective-permute-done.1.refs_5_.refs_1_
  73.4 2.3 %collective-permute-done.2.refs_6_.refs_5_ = f32[256,256]{1,0:T(8,128)} collective-permute-done((f32[256,256]{1,0:T(8,128)S(1)}, f32[256,256]{1,0:T(8,128)}, u32[]{:S(2)}, u32[]{:S(2)}) %collective-permute-start.2) | collective-permute-done | bytes 262176 | tf_op jit(solution)/shard_map/ppermute | solution.py:325
  75.7 5.6 %shard_map.97 = (f32[2,256,512]{2,1,0:T(8,128)S(1)}, f32[2,128,1024]{2,1,0:T(8,128)S(1)}, f32[2,128,1024]{2,1,0:T(8,128)S(1)}) custom-call(s32[1]{0:T(128)} %slice.3.flag_ref, f32[512,128]{1,0:T(8,128)} %get-tuple-element.34.refs_0_, f32[256,256]{1,0:T(8,128)} %copy-done.8, f32[256,256]{1,0:T(8,128)} %get-tuple-element.35.refs_2_.refs_4_, ...), custom_call_target="tpu_custom_call" | custom-call | flops 1409286144 | bytes 5767168 | tf_op jit(solution)/shard_map/pallas_call | solution.py:215
  81.2 0.0 copy-start.6
  81.3 2.1 %collective-permute-start.4 = (f32[2,128,1024]{2,1,0:T(8,128)S(1)}, f32[2,128,1024]{2,1,0:T(8,128)S(1)}, u32[]{:S(2)}, u32[]{:S(2)}) collective-permute-start(f32[2,128,1024]{2,1,0:T(8,128)S(1)} %get-tuple-element.48), channel_id=1, source_target_pairs={{0,1},{1,0},{2,3},{3,2},{4,5},{5,4},{6,7},{7,6},{8,9},{9,8},{10,11... | collective-permute-start | bytes 3145736 | tf_op jit(solution)/shard_map/ppermute | solution.py:299
  83.3 2.6 %collective-permute-start.3 = (f32[2,128,1024]{2,1,0:T(8,128)S(1)}, f32[2,128,1024]{2,1,0:T(8,128)S(1)}, u32[]{:S(2)}, u32[]{:S(2)}) collective-permute-start(f32[2,128,1024]{2,1,0:T(8,128)S(1)} %bitcast.5), channel_id=1, source_target_pairs={{0,1},{1,0},{2,3},{3,2},{4,5},{5,4},{6,7},{7,6},{8,9},{9,8},{10,11... | collective-permute-start | bytes 3145736 | tf_op jit(solution)/shard_map/ppermute | solution.py:299
  85.9 0.0 collective-permute-done.4
  86.0 1.2 add.23
  87.1 0.9 collective-permute-done.3.refs_7_
  88.0 6.7 %shard_map.98 = (f32[512,128]{1,0:T(8,128)}, f32[512,128]{1,0:T(8,128)}, f32[256,256]{1,0:T(8,128)}, f32[256,256]{1,0:T(8,128)}, f32[512,256]{1,0:T(8,128)}) custom-call(s32[1]{0:T(128)} %slice.3.flag_ref, f32[512,128]{1,0:T(8,128)S(1)} %copy-done.10, f32[256,256]{1,0:T(8,128)} %collective-permute-done.1.refs_5_.refs_1_, f32[256,256]{1,0:T(8,128)S(1)} %copy-done.9, ...), custom_call_target="tpu_custom_call" | custom-call | flops 1610612736 | bytes 7077888 | tf_op jit(solution)/shard_map/pallas_call | solution.py:215
  94.7 9.3 %all-to-all-start.2 = ((f32[16,16,1024]{2,1,0:T(8,128)}), f32[16,16,1024]{2,1,0:T(8,128)S(1)}, u32[]{:S(2)}, u32[]{:S(2)}) async-start(f32[16,16,1024]{2,1,0:T(8,128)} %bitcast.3), calls=%async_computation.2 | async-start | bytes 2097152 | tf_op jit(solution)/shard_map/all_to_all | solution.py:319
  104.0 1.9 %collective-permute-start.5 = (f32[256,256]{1,0:T(8,128)S(1)}, f32[256,256]{1,0:T(8,128)S(1)}, u32[]{:S(2)}, u32[]{:S(2)}) collective-permute-start(f32[256,256]{1,0:T(8,128)S(1)} %copy-done.15), channel_id=1, source_target_pairs={{0,32},{32,64},{64,96},{96,128},{128,160},{160,192},{192,224},{224... | collective-permute-start | bytes 786440 | tf_op jit(solution)/shard_map/ppermute | solution.py:325
  105.9 8.7 %collective-permute-start.6 = (f32[256,256]{1,0:T(8,128)S(1)}, f32[256,256]{1,0:T(8,128)S(1)}, u32[]{:S(2)}, u32[]{:S(2)}) collective-permute-start(f32[256,256]{1,0:T(8,128)S(1)} %copy-done.14), channel_id=1, source_target_pairs={{0,480},{32,0},{64,32},{96,64},{128,96},{160,128},{192,160},{224,1... | collective-permute-start | bytes 786440 | tf_op jit(solution)/shard_map/ppermute | solution.py:325
  114.6 0.0 copy-start.1
  114.6 0.0 copy-start.3
  114.6 6.0 %shard_map.99.refs_2_ = f32[512,1024]{1,0:T(8,128)S(1)} custom-call(s32[1]{0:T(128)} %slice.3.flag_ref, f32[512,128]{1,0:T(8,128)} %get-tuple-element.42.refs_0_, f32[512,256]{1,0:T(8,128)} %get-tuple-element.43.refs_1_, f32[512,512]{1,0:T(8,128)} %get-tuple-element.44.refs_2_, f32[512,128]{1,0:T(8,128)} %get-tuple-element.45.refs_3_, ...), custom_call_target="tpu_custom_call" | custom-call | flops 2415919104 | bytes 7602176 | tf_op jit(solution)/shard_map/pallas_call | solution.py:215
  120.7 0.0 collective-permute-done.5.refs_4_
  120.7 10.2 %collective-permute-done.6.refs_5_ = f32[256,256]{1,0:T(8,128)S(1)} collective-permute-done((f32[256,256]{1,0:T(8,128)S(1)}, f32[256,256]{1,0:T(8,128)S(1)}, u32[]{:S(2)}, u32[]{:S(2)}) %collective-permute-start.6) | collective-permute-done | bytes 262176 | tf_op jit(solution)/shard_map/ppermute | solution.py:325
  130.9 1.7 shard_map.100
  132.6 1.9 %collective-permute-start.7 = (f32[2,128,1024]{2,1,0:T(8,128)S(1)}, f32[2,128,1024]{2,1,0:T(8,128)S(1)}, u32[]{:S(2)}, u32[]{:S(2)}) collective-permute-start(f32[2,128,1024]{2,1,0:T(8,128)S(1)} %get-tuple-element.54), channel_id=1, source_target_pairs={{0,1},{1,0},{2,3},{3,2},{4,5},{5,4},{6,7},{7,6},{8,9},{9,8},{10,11... | collective-permute-start | bytes 3145736 | tf_op jit(solution)/shard_map/ppermute | solution.py:299
  134.5 2.6 %collective-permute-done.7 = f32[2,128,1024]{2,1,0:T(8,128)S(1)} collective-permute-done((f32[2,128,1024]{2,1,0:T(8,128)S(1)}, f32[2,128,1024]{2,1,0:T(8,128)S(1)}, u32[]{:S(2)}, u32[]{:S(2)}) %collective-permute-start.7) | collective-permute-done | bytes 1048608 | tf_op jit(solution)/shard_map/ppermute | solution.py:299
  137.2 0.2 add.24
  137.3 0.0 copy-start.12
  137.3 0.0 all-to-all-done.2
  137.4 0.1 reduce_sum.36
  137.4 45.8 %all_to_all.21 = f32[16,16,1024]{2,1,0:T(8,128)S(1)} all-to-all(f32[16,16,1024]{2,1,0:T(8,128)S(1)} %bitcast.8), channel_id=1, replica_groups={{0,2,4,6,8,10,12,14,16,18,20,22,24,26,28,30},{1,3,5,7,9,11,13,15,17,19,..., dimensions={0} | all-to-all | bytes 2097152 | tf_op jit(solution)/shard_map/all_to_all | solution.py:319
  183.3 0.1 reduce_sum.37
  183.3 0.1 multiply_reduce_fusion.1
  183.5 0.7 multiply_subtract_fusion
  (24 shorter events, 0.1 us)
Async XLA Ops:
  0.6 40.4 %copy-start.13 = (f32[16,1024]{1,0:T(8,128)S(1)}, f32[16,1024]{1,0:T(8,128)}, u32[]{:S(2)}) copy-start(f32[16,1024]{1,0:T(8,128)} %param.15) | copy-start | bytes 196612
  41.0 9.8 %copy-start.11 = (f32[16,16,1024]{2,1,0:T(8,128)}, f32[16,16,1024]{2,1,0:T(8,128)S(1)}, u32[]{:S(2)}) copy-start(f32[16,16,1024]{2,1,0:T(8,128)S(1)} %all_to_all.20) | copy-start | bytes 3145732
  41.0 7.1 %copy-start.16 = (s32[2]{0:T(128)S(1)}, s32[2]{0:T(128)}, u32[]{:S(2)}) copy-start(s32[2]{0:T(128)} %param.14) | copy-start | bytes 28
  41.0 9.8 %copy-start.5 = (f32[1024]{0:T(1024)S(1)}, f32[1024]{0:T(1024)}, u32[]{:S(2)}) copy-start(f32[1024]{0:T(1024)} %param.9) | copy-start | bytes 12292
  42.2 31.1 %all-to-all-start.1 = ((f32[16,16,1024]{2,1,0:T(8,128)}), f32[16,16,1024]{2,1,0:T(8,128)S(1)}, u32[]{:S(2)}, u32[]{:S(2)}) async-start(f32[16,16,1024]{2,1,0:T(8,128)} %broadcast_in_dim.8), calls=%async_computation.1 | async-start | bytes 2097152 | tf_op jit(solution)/shard_map/all_to_all | solution.py:311
  46.2 4.5 %collective-permute-start = (f32[2,128,1024]{2,1,0:T(8,128)S(1)}, f32[2,128,1024]{2,1,0:T(8,128)S(1)}, u32[]{:S(2)}, u32[]{:S(2)}) collective-permute-start(f32[2,128,1024]{2,1,0:T(8,128)S(1)} %bitcast.9), channel_id=1, source_target_pairs={{0,1},{1,0},{2,3},{3,2},{4,5},{5,4},{6,7},{7,6},{8,9},{9,8},{10,11... | collective-permute-start | bytes 3145736 | tf_op jit(solution)/shard_map/ppermute | solution.py:299
  50.8 15.6 %copy-start = (f32[1024,256]{1,0:T(8,128)S(1)}, f32[1024,256]{1,0:T(8,128)}, u32[]{:S(2)}) copy-start(f32[1024,256]{1,0:T(8,128)} %refs_0_.3) | copy-start | bytes 3145732
  50.8 15.6 %copy-start.2 = (f32[1024,256]{1,0:T(8,128)S(1)}, f32[1024,256]{1,0:T(8,128)}, u32[]{:S(2)}) copy-start(f32[1024,256]{1,0:T(8,128)} %refs_1_.5) | copy-start | bytes 3145732
  50.8 15.6 %copy-start.7 = (f32[1024,256]{1,0:T(8,128)S(1)}, f32[1024,256]{1,0:T(8,128)}, u32[]{:S(2)}) copy-start(f32[1024,256]{1,0:T(8,128)} %refs_5_.1) | copy-start | bytes 3145732
  56.2 16.5 %copy-start.8 = (f32[256,256]{1,0:T(8,128)}, f32[256,256]{1,0:T(8,128)S(1)}, u32[]{:S(2)}) copy-start(f32[256,256]{1,0:T(8,128)S(1)} %get-tuple-element.36.refs_1_.refs_2_) | copy-start | bytes 786436
  56.3 17.1 %collective-permute-start.1 = (f32[256,256]{1,0:T(8,128)}, f32[256,256]{1,0:T(8,128)}, u32[]{:S(2)}, u32[]{:S(2)}) collective-permute-start(f32[256,256]{1,0:T(8,128)} %get-tuple-element.35.refs_2_.refs_4_), channel_id=1, source_target_pairs={{0,32},{32,64},{64,96},{96,128},{128,160},{160,192},{192,224},{224... | collective-permute-start | bytes 786440 | tf_op jit(solution)/shard_map/ppermute | solution.py:325
  59.7 16.0 %collective-permute-start.2 = (f32[256,256]{1,0:T(8,128)S(1)}, f32[256,256]{1,0:T(8,128)}, u32[]{:S(2)}, u32[]{:S(2)}) collective-permute-start(f32[256,256]{1,0:T(8,128)S(1)} %get-tuple-element.36.refs_1_.refs_2_), channel_id=1, source_target_pairs={{0,480},{32,0},{64,32},{96,64},{128,96},{160,128},{192,160},{224,1... | collective-permute-start | bytes 786440 | tf_op jit(solution)/shard_map/ppermute | solution.py:325
  81.2 6.8 %copy-start.6 = (f32[256,1024]{1,0:T(8,128)S(1)}, f32[256,1024]{1,0:T(8,128)}, u32[]{:S(2)}) copy-start(f32[256,1024]{1,0:T(8,128)} %refs_8_.1) | copy-start | bytes 3145732
  81.2 6.8 %copy-start.9 = (f32[256,256]{1,0:T(8,128)S(1)}, f32[256,256]{1,0:T(8,128)}, u32[]{:S(2)}) copy-start(f32[256,256]{1,0:T(8,128)} %copy-done.8) | copy-start | bytes 786436
  81.3 6.8 %copy-start.10 = (f32[512,128]{1,0:T(8,128)S(1)}, f32[512,128]{1,0:T(8,128)}, u32[]{:S(2)}) copy-start(f32[512,128]{1,0:T(8,128)} %get-tuple-element.34.refs_0_) | copy-start | bytes 786436
  81.3 4.7 %collective-permute-start.4 = (f32[2,128,1024]{2,1,0:T(8,128)S(1)}, f32[2,128,1024]{2,1,0:T(8,128)S(1)}, u32[]{:S(2)}, u32[]{:S(2)}) collective-permute-start(f32[2,128,1024]{2,1,0:T(8,128)S(1)} %get-tuple-element.48), channel_id=1, source_target_pairs={{0,1},{1,0},{2,3},{3,2},{4,5},{5,4},{6,7},{7,6},{8,9},{9,8},{10,11... | collective-permute-start | bytes 3145736 | tf_op jit(solution)/shard_map/ppermute | solution.py:299
  83.3 4.7 %collective-permute-start.3 = (f32[2,128,1024]{2,1,0:T(8,128)S(1)}, f32[2,128,1024]{2,1,0:T(8,128)S(1)}, u32[]{:S(2)}, u32[]{:S(2)}) collective-permute-start(f32[2,128,1024]{2,1,0:T(8,128)S(1)} %bitcast.5), channel_id=1, source_target_pairs={{0,1},{1,0},{2,3},{3,2},{4,5},{5,4},{6,7},{7,6},{8,9},{9,8},{10,11... | collective-permute-start | bytes 3145736 | tf_op jit(solution)/shard_map/ppermute | solution.py:299
  94.7 9.3 %copy-start.15 = (f32[256,256]{1,0:T(8,128)S(1)}, f32[256,256]{1,0:T(8,128)}, u32[]{:S(2)}) copy-start(f32[256,256]{1,0:T(8,128)} %get-tuple-element.51) | copy-start | bytes 786436
  94.7 11.2 %copy-start.14 = (f32[256,256]{1,0:T(8,128)S(1)}, f32[256,256]{1,0:T(8,128)}, u32[]{:S(2)}) copy-start(f32[256,256]{1,0:T(8,128)} %get-tuple-element.52) | copy-start | bytes 786436
  94.7 42.7 %all-to-all-start.2 = ((f32[16,16,1024]{2,1,0:T(8,128)}), f32[16,16,1024]{2,1,0:T(8,128)S(1)}, u32[]{:S(2)}, u32[]{:S(2)}) async-start(f32[16,16,1024]{2,1,0:T(8,128)} %bitcast.3), calls=%async_computation.2 | async-start | bytes 2097152 | tf_op jit(solution)/shard_map/all_to_all | solution.py:319
  104.0 16.7 %collective-permute-start.5 = (f32[256,256]{1,0:T(8,128)S(1)}, f32[256,256]{1,0:T(8,128)S(1)}, u32[]{:S(2)}, u32[]{:S(2)}) collective-permute-start(f32[256,256]{1,0:T(8,128)S(1)} %copy-done.15), channel_id=1, source_target_pairs={{0,32},{32,64},{64,96},{96,128},{128,160},{160,192},{192,224},{224... | collective-permute-start | bytes 786440 | tf_op jit(solution)/shard_map/ppermute | solution.py:325
  105.9 25.0 %collective-permute-start.6 = (f32[256,256]{1,0:T(8,128)S(1)}, f32[256,256]{1,0:T(8,128)S(1)}, u32[]{:S(2)}, u32[]{:S(2)}) collective-permute-start(f32[256,256]{1,0:T(8,128)S(1)} %copy-done.14), channel_id=1, source_target_pairs={{0,480},{32,0},{64,32},{96,64},{128,96},{160,128},{192,160},{224,1... | collective-permute-start | bytes 786440 | tf_op jit(solution)/shard_map/ppermute | solution.py:325
  114.6 16.3 %copy-start.1 = (f32[1024,256]{1,0:T(8,128)S(1)}, f32[1024,256]{1,0:T(8,128)}, u32[]{:S(2)}) copy-start(f32[1024,256]{1,0:T(8,128)} %refs_0_.3) | copy-start | bytes 3145732
  114.6 16.3 %copy-start.3 = (f32[1024,256]{1,0:T(8,128)S(1)}, f32[1024,256]{1,0:T(8,128)}, u32[]{:S(2)}) copy-start(f32[1024,256]{1,0:T(8,128)} %refs_1_.5) | copy-start | bytes 3145732
  114.6 16.3 %copy-start.4 = (f32[512,256]{1,0:T(8,128)S(1)}, f32[512,256]{1,0:T(8,128)}, u32[]{:S(2)}) copy-start(f32[512,256]{1,0:T(8,128)} %get-tuple-element.50.refs_3_) | copy-start | bytes 1572868
  132.6 4.6 %collective-permute-start.7 = (f32[2,128,1024]{2,1,0:T(8,128)S(1)}, f32[2,128,1024]{2,1,0:T(8,128)S(1)}, u32[]{:S(2)}, u32[]{:S(2)}) collective-permute-start(f32[2,128,1024]{2,1,0:T(8,128)S(1)} %get-tuple-element.54), channel_id=1, source_target_pairs={{0,1},{1,0},{2,3},{3,2},{4,5},{5,4},{6,7},{7,6},{8,9},{9,8},{10,11... | collective-permute-start | bytes 3145736 | tf_op jit(solution)/shard_map/ppermute | solution.py:299
  137.3 46.0 %copy-start.12 = (f32[16,1024]{1,0:T(8,128)S(1)}, f32[16,1024]{1,0:T(8,128)}, u32[]{:S(2)}) copy-start(f32[16,1024]{1,0:T(8,128)} %param.8) | copy-start | bytes 196612

commit v4 on v3

--- a/solution.py
+++ b/solution.py
@@ -291,7 +291,19 @@
     )
 
 
+def halves_kernel(flag_ref, mine_ref, other_ref, kept_ref, given_ref):
+    place = lax.axis_index("head") // 2 % 2
+    kept_ref[...] = mine_ref[:, place] + other_ref[:, place]
+    given_ref[...] = mine_ref[:, 1 - place] + other_ref[:, 1 - place]
+
+
+def halves_call(flag, mine, other):
+    lines, _, rows, width = mine.shape
+    return call(halves_kernel, [(lines, rows, width)] * 2, flag, [mine, other], flops=mine.size)
+
+
 CHIP = 2
+PAIR = 2
 
 
 def core_swap(x):
@@ -317,6 +329,18 @@
     chips = len(groups[0])
     split = part.reshape(chips, -1, part.shape[2])
     swapped = lax.all_to_all(split, "head", 0, 0, tiled=True, axis_index_groups=groups)
+    return jnp.sum(swapped, axis=0)
+
+
+def pair_swap(x):
+    length = lax.axis_size("head")
+    return lax.ppermute(x, "head", [(i, i ^ CHIP) for i in range(length)])
+
+
+def sum_line(part):
+    length, step = lax.axis_size("head"), CHIP * PAIR
+    groups = [list(range(place, length, step)) for place in range(step)]
+    swapped = lax.all_to_all(part, "head", 0, 0, tiled=True, axis_index_groups=groups)
     return jnp.sum(swapped, axis=0)
 
 
@@ -337,14 +361,17 @@
     low, high = along(last, 1), along(first, -1)
     query_moved, query_still, kv_still, probs_still, out_still = still_call(scale, flag, parts, w_query, w_key, w_value)
     cot_own, out_still = lax.optimization_barrier((cot_own, out_still))
-    cot_other = core_swap(cot_own)
+    out_still, cot_other = lax.optimization_barrier((out_still, core_swap(cot_own)))
     probs_moved, mine, theirs = moved_call(scale, flag, query_moved, first, last, low, high, out_still, w_out)
-    out_part = mine + core_swap(theirs)
+    lines = (lax.axis_size("head") // (CHIP * PAIR), PAIR, -1, tokens.shape[1])
+    kept, given = halves_call(flag, mine.reshape(lines), core_swap(theirs).reshape(lines))
+    received = pair_swap(given)
     grad_still, grad_query, left, right, keep = moved_back_call(
         scale, flag, cot_own, cot_other, w_out, query_moved, first, last, low, high, probs_moved
     )
+    out_part = kept + received
     grad_query, out_part = lax.optimization_barrier((grad_query, out_part))
-    out_sum = sum_chips(out_part)
+    out_sum = sum_line(out_part)
     from_left, from_right = along(right, 1), along(left, -1)
     terms = still_back_call(
         scale, flag, grad_still, query_still, kv_still, probs_still, grad_query, w_query, w_key, w_value

time: 185 us -> 199 us (1.076)
  the two profiles are of different devices: /device:TPU:40 before, /device:TPU:6 now
where the time goes in v4:
time: 199 us; the launch traced here: 197 us
  blocking collectives  91.7 us (46%)
  waiting for transfers between devices  42 us (21%)
  Pallas kernels  29.7 us (15%)
  starting transfers between devices  27.1 us (14%)
  local copies, waits for them, and re-layouts  2.82 us (1%)
  other arithmetic  2.46 us (1%)
    all_to_all x1, blocking collectives, gather_chips(): lax.all_to_all(sent, 'head', 0, 0, tiled=True, axis_index_groups=groups)  39.4 us
    all_to_all x1, blocking collectives, sum_chips(): lax.all_to_all(split, 'head', 0, 0, tiled=True, axis_index_groups=groups)  31.4 us
    pallas_call x7, Pallas kernels, call(): pl.pallas_call(body, out_shape=[pltpu.HBM(x.shape, x.dtype) for x in out]...  29.7 us
    all_to_all x1, blocking collectives, sum_line(): lax.all_to_all(part, 'head', 0, 0, tiled=True, axis_index_groups=groups)  20.8 us
    ppermute x4, waiting for transfers between devices, along(): lax.ppermute(x, 'ctx', [(i, (i + by) % length) for i in range(length)])  19.3 us
    ppermute x4, starting transfers between devices, along(): lax.ppermute(x, 'ctx', [(i, (i + by) % length) for i in range(length)])  12.2 us
    all_to_all x1, waiting for transfers between devices, gather_chips(): lax.all_to_all(sent, 'head', 0, 0, tiled=True, axis_index_groups=groups)  11.7 us
    ppermute x4, starting transfers between devices, core_swap(): return lax.ppermute(x, 'head', [(i, i ^ 1) for i in range(length)])  7.8 us
  transfers between devices with their start and end apart: 10, of which 7 were waited for; matrix products, arithmetic and copies ran while one was open for 0% of the time, Pallas kernels for 12%

profile of v4, /device:TPU:6, one launch (start us, length us, event | category | flops | bytes accessed | tf_op | source)
XLA Modules:
  0.0 196.7 jit_solution(14767944758845120407)
XLA Ops:
  0.6 1.0 broadcast_in_dim.6
  1.6 39.4 %all_to_all.20 = f32[16,16,1024]{2,1,0:T(8,128)S(1)} all-to-all(f32[16,16,1024]{2,1,0:T(8,128)S(1)} %broadcast_in_dim.6), channel_id=1, replica_groups={{0,2,4,6,8,10,12,14,16,18,20,22,24,26,28,30},{1,3,5,7,9,11,13,15,17,19,..., dimensions={0} | all-to-all | bytes 2097152 | tf_op jit(solution)/shard_map/all_to_all | solution.py:323
  41.1 0.0 copy-done.15
  41.1 1.2 broadcast_in_dim.8
  42.3 3.7 %all-to-all-start.1 = ((f32[16,16,1024]{2,1,0:T(8,128)}), f32[16,16,1024]{2,1,0:T(8,128)S(1)}, u32[]{:S(2)}, u32[]{:S(2)}) async-start(f32[16,16,1024]{2,1,0:T(8,128)} %broadcast_in_dim.8), calls=%async_computation.1 | async-start | bytes 2097152 | tf_op jit(solution)/shard_map/all_to_all | solution.py:323
  45.9 1.9 collective-permute-start
  47.8 0.0 copy-done.16
  47.9 0.6 slice.3.flag_ref
  48.4 2.0 %collective-permute-done.refs_3_ = f32[2,128,1024]{2,1,0:T(8,128)S(1)} collective-permute-done((f32[2,128,1024]{2,1,0:T(8,128)S(1)}, f32[2,128,1024]{2,1,0:T(8,128)S(1)}, u32[]{:S(2)}, u32[]{:S(2)}) %collective-permute-start) | collective-permute-done | bytes 1048608 | tf_op jit(solution)/shard_map/ppermute | solution.py:311
  50.5 0.0 copy-start.7
  50.5 4.8 %shard_map.95 = (f32[256,256]{1,0:T(8,128)S(1)}, f32[256,256]{1,0:T(8,128)S(1)}, bf16[512,1024]{1,0:T(8,128)(2,1)S(1)}, bf16[512,1024]{1,0:T(8,128)(2,1)S(1)}, bf16[512,1024]{1,0:T(8,128)(2,1)S(1)}) custom-call(s32[1]{0:T(128)} %slice.3.flag_ref, f32[2,128,1024]{2,1,0:T(8,128)} %bitcast.13, f32[1024,256]{1,0:T(8,128)} %refs_0_.3, f32[1024,256]{1,0:T(8,128)} %refs_1_.5, ...), custom_call_target="tpu_custom_call" | custom-call | flops 1610612736 | bytes 7868416 | tf_op jit(solution)/shard_map/pallas_call | solution.py:215
  55.3 6.3 %shard_map.96 = (f32[512,128]{1,0:T(8,128)}, f32[512,128]{1,0:T(8,128)}, f32[512,256]{1,0:T(8,128)}, f32[512,512]{1,0:T(8,128)}, f32[512,128]{1,0:T(8,128)}) custom-call(s32[1]{0:T(128)} %slice.3.flag_ref, f32[1024,256]{1,0:T(8,128)S(1)} %copy-done, f32[1024,256]{1,0:T(8,128)S(1)} %copy-done.2, f32[1024,256]{1,0:T(8,128)S(1)} %copy-done.7, ...), custom_call_target="tpu_custom_call" | custom-call | flops 3825205248 | bytes 8650752 | tf_op jit(solution)/shard_map/pallas_call | solution.py:215
  61.7 11.7 %all-to-all-done.1 = f32[16,16,1024]{2,1,0:T(8,128)S(1)} async-done(((f32[16,16,1024]{2,1,0:T(8,128)}), f32[16,16,1024]{2,1,0:T(8,128)S(1)}, u32[]{:S(2)}, u32[]{:S(2)}) %all-to-all-start.1) | async-done | bytes 1048608 | tf_op jit(solution)/shard_map/all_to_all | solution.py:323
  73.4 1.9 collective-permute-start.2
  75.3 4.4 %collective-permute-start.1 = (f32[256,256]{1,0:T(8,128)S(1)}, f32[256,256]{1,0:T(8,128)S(1)}, u32[]{:S(2)}, u32[]{:S(2)}) collective-permute-start(f32[256,256]{1,0:T(8,128)S(1)} %get-tuple-element.39.refs_2_.refs_4_), channel_id=1, source_target_pairs={{0,32},{32,64},{64,96},{96,128},{128,160},{160,192},{192,224},{224... | collective-permute-start | bytes 786440 | tf_op jit(solution)/shard_map/ppermute | solution.py:349
  79.7 1.9 collective-permute-start.3
  81.6 0.0 collective-permute-done.2.refs_7_
  81.7 4.4 %collective-permute-done.1.refs_5_.refs_1_ = f32[256,256]{1,0:T(8,128)S(1)} collective-permute-done((f32[256,256]{1,0:T(8,128)S(1)}, f32[256,256]{1,0:T(8,128)S(1)}, u32[]{:S(2)}, u32[]{:S(2)}) %collective-permute-start.1) | collective-permute-done | bytes 262176 | tf_op jit(solution)/shard_map/ppermute | solution.py:349
  86.0 12.4 %collective-permute-done.3.refs_6_.refs_5_ = f32[256,256]{1,0:T(8,128)S(1)} collective-permute-done((f32[256,256]{1,0:T(8,128)S(1)}, f32[256,256]{1,0:T(8,128)S(1)}, u32[]{:S(2)}, u32[]{:S(2)}) %collective-permute-start.3) | collective-permute-done | bytes 262176 | tf_op jit(solution)/shard_map/ppermute | solution.py:349
  98.4 4.5 %shard_map.97 = (f32[2,256,512]{2,1,0:T(8,128)S(1)}, f32[2,128,1024]{2,1,0:T(8,128)S(1)}, f32[2,128,1024]{2,1,0:T(8,128)S(1)}) custom-call(s32[1]{0:T(128)} %slice.3.flag_ref, f32[512,128]{1,0:T(8,128)} %get-tuple-element.38.refs_0_, f32[256,256]{1,0:T(8,128)} %copy-done.8, f32[256,256]{1,0:T(8,128)} %copy-done.10, f32[256,1024]{1,0:T(8,128)} %refs_8_.1, ...), custom_call_target="tpu_custom_call" | custom-call | flops 1409286144 | bytes 5767168 | tf_op jit(solution)/shard_map/pallas_call | solution.py:215
  103.0 0.0 copy-start.6
  103.0 0.0 copy-start.9
  103.0 0.0 copy-start.11
  103.0 0.0 copy-start.12
  103.0 2.1 %collective-permute-start.4 = (f32[2,128,1024]{2,1,0:T(8,128)S(1)}, f32[2,128,1024]{2,1,0:T(8,128)S(1)}, u32[]{:S(2)}, u32[]{:S(2)}) collective-permute-start(f32[2,128,1024]{2,1,0:T(8,128)S(1)} %get-tuple-element.54), channel_id=1, source_target_pairs={{0,1},{1,0},{2,3},{3,2},{4,5},{5,4},{6,7},{7,6},{8,9},{9,8},{10,11... | collective-permute-start | bytes 3145736 | tf_op jit(solution)/shard_map/ppermute | solution.py:311
  105.1 2.6 %collective-permute-done.4 = f32[2,128,1024]{2,1,0:T(8,128)S(1)} collective-permute-done((f32[2,128,1024]{2,1,0:T(8,128)S(1)}, f32[2,128,1024]{2,1,0:T(8,128)S(1)}, u32[]{:S(2)}, u32[]{:S(2)}) %collective-permute-start.4) | collective-permute-done | bytes 1048608 | tf_op jit(solution)/shard_map/ppermute | solution.py:311
  107.7 0.8 shard_map.99
  108.5 3.4 %collective-permute-start.5 = (f32[8,16,1024]{2,1,0:T(8,128)S(1)}, f32[8,16,1024]{2,1,0:T(8,128)S(1)}, u32[]{:S(2)}, u32[]{:S(2)}) collective-permute-start(f32[8,16,1024]{2,1,0:T(8,128)S(1)} %get-tuple-element.56), channel_id=1, source_target_pairs={{0,2},{1,3},{2,0},{3,1},{4,6},{5,7},{6,4},{7,5},{8,10},{9,11},{10,... | collective-permute-start | bytes 1572872 | tf_op jit(solution)/shard_map/ppermute | solution.py:337
  111.9 5.5 %shard_map.98 = (f32[512,128]{1,0:T(8,128)}, f32[512,128]{1,0:T(8,128)}, f32[256,256]{1,0:T(8,128)}, f32[256,256]{1,0:T(8,128)}, f32[512,256]{1,0:T(8,128)}) custom-call(s32[1]{0:T(128)} %slice.3.flag_ref, f32[512,128]{1,0:T(8,128)S(1)} %copy-done.12, f32[256,256]{1,0:T(8,128)S(1)} %collective-permute-done.1.refs_5_.refs_1_, f32[256,256]{1,0:T(8,128)S(1)} %copy-done.9, ...), custom_call_target="tpu_custom_call" | custom-call | flops 1610612736 | bytes 7077888 | tf_op jit(solution)/shard_map/pallas_call | solution.py:215
  117.5 1.9 collective-permute-start.6
  119.4 3.9 %collective-permute-start.7 = (f32[256,256]{1,0:T(8,128)}, f32[256,256]{1,0:T(8,128)S(1)}, u32[]{:S(2)}, u32[]{:S(2)}) collective-permute-start(f32[256,256]{1,0:T(8,128)} %get-tuple-element.60), channel_id=1, source_target_pairs={{0,480},{32,0},{64,32},{96,64},{128,96},{160,128},{192,160},{224,1... | collective-permute-start | bytes 786440 | tf_op jit(solution)/shard_map/ppermute | solution.py:349
  123.3 6.3 %collective-permute-done.5 = f32[8,16,1024]{2,1,0:T(8,128)S(1)} collective-permute-done((f32[8,16,1024]{2,1,0:T(8,128)S(1)}, f32[8,16,1024]{2,1,0:T(8,128)S(1)}, u32[]{:S(2)}, u32[]{:S(2)}) %collective-permute-start.5) | collective-permute-done | bytes 524320 | tf_op jit(solution)/shard_map/ppermute | solution.py:337
  129.6 0.1 add.23
  129.7 0.0 copy-start.1
  129.7 0.0 copy-start.3
  129.7 6.0 %shard_map.100.refs_2_ = f32[512,1024]{1,0:T(8,128)S(1)} custom-call(s32[1]{0:T(128)} %slice.3.flag_ref, f32[512,128]{1,0:T(8,128)} %get-tuple-element.48.refs_0_, f32[512,256]{1,0:T(8,128)} %get-tuple-element.49.refs_1_, f32[512,512]{1,0:T(8,128)} %get-tuple-element.50.refs_2_, f32[512,128]{1,0:T(8,128)} %get-tuple-element.51.refs_3_, ...), custom_call_target="tpu_custom_call" | custom-call | flops 2415919104 | bytes 7602176 | tf_op jit(solution)/shard_map/pallas_call | solution.py:215
  135.8 0.0 collective-permute-done.6.refs_4_
  135.8 2.6 %collective-permute-done.7.refs_5_ = f32[256,256]{1,0:T(8,128)S(1)} collective-permute-done((f32[256,256]{1,0:T(8,128)}, f32[256,256]{1,0:T(8,128)S(1)}, u32[]{:S(2)}, u32[]{:S(2)}) %collective-permute-start.7) | collective-permute-done | bytes 262176 | tf_op jit(solution)/shard_map/ppermute | solution.py:349
  138.4 1.7 shard_map.101
  140.1 1.9 collective-permute-start.8
  142.0 20.8 %all_to_all.21 = f32[8,16,1024]{2,1,0:T(8,128)S(1)} all-to-all(f32[8,16,1024]{2,1,0:T(8,128)S(1)} %add.23), channel_id=1, replica_groups={{0,4,8,12,16,20,24,28},{1,5,9,13,17,21,25,29},{2,6,10,14,18,22,26,30},{..., dimensions={0} | all-to-all | bytes 1048576 | tf_op jit(solution)/shard_map/all_to_all | solution.py:343
  162.9 0.0 collective-permute-done.8
  162.9 1.4 add.24
  164.3 0.0 copy-start.14
  164.3 31.4 %all_to_all.22 = f32[16,16,1024]{2,1,0:T(8,128)S(1)} all-to-all(f32[16,16,1024]{2,1,0:T(8,128)S(1)} %bitcast.11), channel_id=1, replica_groups={{0,2,4,6,8,10,12,14,16,18,20,22,24,26,28,30},{1,3,5,7,9,11,13,15,17,19,..., dimensions={0} | all-to-all | bytes 2097152 | tf_op jit(solution)/shard_map/all_to_all | solution.py:331
  195.8 0.1 reduce_sum.37
  195.8 0.1 multiply_reduce_fusion.1
  196.0 0.7 multiply_subtract_fusion
  (26 shorter events, 0.1 us)
Async XLA Ops:
  0.6 40.4 %copy-start.15 = (f32[16,1024]{1,0:T(8,128)S(1)}, f32[16,1024]{1,0:T(8,128)}, u32[]{:S(2)}) copy-start(f32[16,1024]{1,0:T(8,128)} %param.15) | copy-start | bytes 196612
  41.1 9.4 %copy-start.13 = (f32[16,16,1024]{2,1,0:T(8,128)}, f32[16,16,1024]{2,1,0:T(8,128)S(1)}, u32[]{:S(2)}) copy-start(f32[16,16,1024]{2,1,0:T(8,128)S(1)} %all_to_all.20) | copy-start | bytes 3145732
  41.1 6.8 %copy-start.16 = (s32[2]{0:T(128)S(1)}, s32[2]{0:T(128)}, u32[]{:S(2)}) copy-start(s32[2]{0:T(128)} %param.14) | copy-start | bytes 28
  41.1 9.4 %copy-start.5 = (f32[1024]{0:T(1024)S(1)}, f32[1024]{0:T(1024)}, u32[]{:S(2)}) copy-start(f32[1024]{0:T(1024)} %param.9) | copy-start | bytes 12292
  42.3 31.1 %all-to-all-start.1 = ((f32[16,16,1024]{2,1,0:T(8,128)}), f32[16,16,1024]{2,1,0:T(8,128)S(1)}, u32[]{:S(2)}, u32[]{:S(2)}) async-start(f32[16,16,1024]{2,1,0:T(8,128)} %broadcast_in_dim.8), calls=%async_computation.1 | async-start | bytes 2097152 | tf_op jit(solution)/shard_map/all_to_all | solution.py:323
  45.9 4.6 %collective-permute-start = (f32[2,128,1024]{2,1,0:T(8,128)S(1)}, f32[2,128,1024]{2,1,0:T(8,128)S(1)}, u32[]{:S(2)}, u32[]{:S(2)}) collective-permute-start(f32[2,128,1024]{2,1,0:T(8,128)S(1)} %bitcast.12), channel_id=1, source_target_pairs={{0,1},{1,0},{2,3},{3,2},{4,5},{5,4},{6,7},{7,6},{8,9},{9,8},{10,11... | collective-permute-start | bytes 3145736 | tf_op jit(solution)/shard_map/ppermute | solution.py:311
  50.5 4.8 %copy-start = (f32[1024,256]{1,0:T(8,128)S(1)}, f32[1024,256]{1,0:T(8,128)}, u32[]{:S(2)}) copy-start(f32[1024,256]{1,0:T(8,128)} %refs_0_.3) | copy-start | bytes 3145732
  50.5 4.8 %copy-start.2 = (f32[1024,256]{1,0:T(8,128)S(1)}, f32[1024,256]{1,0:T(8,128)}, u32[]{:S(2)}) copy-start(f32[1024,256]{1,0:T(8,128)} %refs_1_.5) | copy-start | bytes 3145732
  50.5 4.8 %copy-start.7 = (f32[1024,256]{1,0:T(8,128)S(1)}, f32[1024,256]{1,0:T(8,128)}, u32[]{:S(2)}) copy-start(f32[1024,256]{1,0:T(8,128)} %refs_5_.1) | copy-start | bytes 3145732
  55.3 20.0 %copy-start.10 = (f32[256,256]{1,0:T(8,128)}, f32[256,256]{1,0:T(8,128)S(1)}, u32[]{:S(2)}) copy-start(f32[256,256]{1,0:T(8,128)S(1)} %get-tuple-element.39.refs_2_.refs_4_) | copy-start | bytes 786436
  55.3 24.4 %copy-start.8 = (f32[256,256]{1,0:T(8,128)}, f32[256,256]{1,0:T(8,128)S(1)}, u32[]{:S(2)}) copy-start(f32[256,256]{1,0:T(8,128)S(1)} %get-tuple-element.40.refs_1_.refs_2_) | copy-start | bytes 786436
  73.4 8.3 %collective-permute-start.2 = (f32[2,128,1024]{2,1,0:T(8,128)S(1)}, f32[2,128,1024]{2,1,0:T(8,128)S(1)}, u32[]{:S(2)}, u32[]{:S(2)}) collective-permute-start(f32[2,128,1024]{2,1,0:T(8,128)S(1)} %bitcast.8), channel_id=1, source_target_pairs={{0,1},{1,0},{2,3},{3,2},{4,5},{5,4},{6,7},{7,6},{8,9},{9,8},{10,11... | collective-permute-start | bytes 3145736 | tf_op jit(solution)/shard_map/ppermute | solution.py:311
  75.3 10.7 %collective-permute-start.1 = (f32[256,256]{1,0:T(8,128)S(1)}, f32[256,256]{1,0:T(8,128)S(1)}, u32[]{:S(2)}, u32[]{:S(2)}) collective-permute-start(f32[256,256]{1,0:T(8,128)S(1)} %get-tuple-element.39.refs_2_.refs_4_), channel_id=1, source_target_pairs={{0,32},{32,64},{64,96},{96,128},{128,160},{160,192},{192,224},{224... | collective-permute-start | bytes 786440 | tf_op jit(solution)/shard_map/ppermute | solution.py:349
  79.7 18.7 %collective-permute-start.3 = (f32[256,256]{1,0:T(8,128)S(1)}, f32[256,256]{1,0:T(8,128)S(1)}, u32[]{:S(2)}, u32[]{:S(2)}) collective-permute-start(f32[256,256]{1,0:T(8,128)S(1)} %get-tuple-element.40.refs_1_.refs_2_), channel_id=1, source_target_pairs={{0,480},{32,0},{64,32},{96,64},{128,96},{160,128},{192,160},{224,1... | collective-permute-start | bytes 786440 | tf_op jit(solution)/shard_map/ppermute | solution.py:349
  103.0 8.9 %copy-start.6 = (f32[256,1024]{1,0:T(8,128)S(1)}, f32[256,1024]{1,0:T(8,128)}, u32[]{:S(2)}) copy-start(f32[256,1024]{1,0:T(8,128)} %refs_8_.1) | copy-start | bytes 3145732
  103.0 8.9 %copy-start.9 = (f32[256,256]{1,0:T(8,128)S(1)}, f32[256,256]{1,0:T(8,128)}, u32[]{:S(2)}) copy-start(f32[256,256]{1,0:T(8,128)} %copy-done.8) | copy-start | bytes 786436
  103.0 8.9 %copy-start.11 = (f32[256,256]{1,0:T(8,128)S(1)}, f32[256,256]{1,0:T(8,128)}, u32[]{:S(2)}) copy-start(f32[256,256]{1,0:T(8,128)} %copy-done.10) | copy-start | bytes 786436
  103.0 8.9 %copy-start.12 = (f32[512,128]{1,0:T(8,128)S(1)}, f32[512,128]{1,0:T(8,128)}, u32[]{:S(2)}) copy-start(f32[512,128]{1,0:T(8,128)} %get-tuple-element.38.refs_0_) | copy-start | bytes 786436
  103.0 4.7 %collective-permute-start.4 = (f32[2,128,1024]{2,1,0:T(8,128)S(1)}, f32[2,128,1024]{2,1,0:T(8,128)S(1)}, u32[]{:S(2)}, u32[]{:S(2)}) collective-permute-start(f32[2,128,1024]{2,1,0:T(8,128)S(1)} %get-tuple-element.54), channel_id=1, source_target_pairs={{0,1},{1,0},{2,3},{3,2},{4,5},{5,4},{6,7},{7,6},{8,9},{9,8},{10,11... | collective-permute-start | bytes 3145736 | tf_op jit(solution)/shard_map/ppermute | solution.py:311
  108.5 21.2 %collective-permute-start.5 = (f32[8,16,1024]{2,1,0:T(8,128)S(1)}, f32[8,16,1024]{2,1,0:T(8,128)S(1)}, u32[]{:S(2)}, u32[]{:S(2)}) collective-permute-start(f32[8,16,1024]{2,1,0:T(8,128)S(1)} %get-tuple-element.56), channel_id=1, source_target_pairs={{0,2},{1,3},{2,0},{3,1},{4,6},{5,7},{6,4},{7,5},{8,10},{9,11},{10,... | collective-permute-start | bytes 1572872 | tf_op jit(solution)/shard_map/ppermute | solution.py:337
  117.5 18.3 %collective-permute-start.6 = (f32[256,256]{1,0:T(8,128)}, f32[256,256]{1,0:T(8,128)S(1)}, u32[]{:S(2)}, u32[]{:S(2)}) collective-permute-start(f32[256,256]{1,0:T(8,128)} %get-tuple-element.59), channel_id=1, source_target_pairs={{0,32},{32,64},{64,96},{96,128},{128,160},{160,192},{192,224},{224... | collective-permute-start | bytes 786440 | tf_op jit(solution)/shard_map/ppermute | solution.py:349
  119.4 18.9 %collective-permute-start.7 = (f32[256,256]{1,0:T(8,128)}, f32[256,256]{1,0:T(8,128)S(1)}, u32[]{:S(2)}, u32[]{:S(2)}) collective-permute-start(f32[256,256]{1,0:T(8,128)} %get-tuple-element.60), channel_id=1, source_target_pairs={{0,480},{32,0},{64,32},{96,64},{128,96},{160,128},{192,160},{224,1... | collective-permute-start | bytes 786440 | tf_op jit(solution)/shard_map/ppermute | solution.py:349
  129.7 8.6 %copy-start.1 = (f32[1024,256]{1,0:T(8,128)S(1)}, f32[1024,256]{1,0:T(8,128)}, u32[]{:S(2)}) copy-start(f32[1024,256]{1,0:T(8,128)} %refs_0_.3) | copy-start | bytes 3145732
  129.7 8.6 %copy-start.3 = (f32[1024,256]{1,0:T(8,128)S(1)}, f32[1024,256]{1,0:T(8,128)}, u32[]{:S(2)}) copy-start(f32[1024,256]{1,0:T(8,128)} %refs_1_.5) | copy-start | bytes 3145732
  129.7 8.6 %copy-start.4 = (f32[512,256]{1,0:T(8,128)S(1)}, f32[512,256]{1,0:T(8,128)}, u32[]{:S(2)}) copy-start(f32[512,256]{1,0:T(8,128)} %get-tuple-element.58.refs_3_) | copy-start | bytes 1572868
  140.1 22.8 %collective-permute-start.8 = (f32[2,128,1024]{2,1,0:T(8,128)S(1)}, f32[2,128,1024]{2,1,0:T(8,128)}, u32[]{:S(2)}, u32[]{:S(2)}) collective-permute-start(f32[2,128,1024]{2,1,0:T(8,128)S(1)} %get-tuple-element.62), channel_id=1, source_target_pairs={{0,1},{1,0},{2,3},{3,2},{4,5},{5,4},{6,7},{7,6},{8,9},{9,8},{10,11... | collective-permute-start | bytes 3145736 | tf_op jit(solution)/shard_map/ppermute | solution.py:311
  164.3 31.5 %copy-start.14 = (f32[16,1024]{1,0:T(8,128)S(1)}, f32[16,1024]{1,0:T(8,128)}, u32[]{:S(2)}) copy-start(f32[16,1024]{1,0:T(8,128)} %param.8) | copy-start | bytes 196612
